TPU v7x, 128 devices: a whole 4x4x4 slice. The times are simulated.
128 devices in a mesh: seq: 32 (over y, z, core), exp: 4 (over x).
Axes of the slice: x: 4, y: 4, z: 4, core: 2. Of those that a mesh axis runs over, the one named last changes fastest.
Arguments:
- query_proj: bfloat16 [8192, 2048], P('seq', 'exp'), may hold values from -6 to 6
- key_proj: bfloat16 [8192, 2048], P('seq', 'exp'), may hold values from -6 to 6
- value_proj: bfloat16 [8192, 4096], P('seq', 'exp'), may hold values from -6 to 6
- result_valve_maps: bfloat16 [8192, 4096], P('seq', 'exp'), may hold values from -6 to 6
- beta_logit: float32 [8192, 32], P('seq', 'exp'), may hold values from -12 to 3
- decay_logit: float32 [8192, 32], P('seq', 'exp'), may hold values from -8 to 16414
- decay_rate: float32 [32], P('exp'), may hold values from 0 to 0.06
- conv_query: float32 [4, 2048], P(None, 'exp'), may hold values from -3 to 3
- conv_key: float32 [4, 2048], P(None, 'exp'), may hold values from -3 to 3
- conv_value: float32 [4, 4096], P(None, 'exp'), may hold values from -3 to 3
- norm_gain: float32 [128], replicated, may hold values from 0.1 to 1.9
- output_weight: bfloat16 [4096, 2048], P('exp'), may hold values from -0.09375 to 0.09375
- residual: bfloat16 [8192, 2048], P(('seq', 'exp')), may hold values from -6 to 6
- post_gain: float32 [2048], replicated, may hold values from 0.1 to 1.9
- route_experts: int32 [8192, 10], P(('seq', 'exp')), may hold values from 0 to 255, all different within a row; in each aligned block of 64 rows (0 to 63, 64 to 127, ...) at most 6 rows name the same one
- route_weights: float32 [8192, 10], P(('seq', 'exp')), may hold values from 0.05 to 1
- expert_gate: bfloat16 [256, 2048, 512], P(('seq', 'exp')), may hold values from -0.125 to 0.125
- expert_up: bfloat16 [256, 2048, 512], P(('seq', 'exp')), may hold values from -0.125 to 0.125
- expert_down: bfloat16 [256, 512, 2048], P(('seq', 'exp')), may hold values from -0.25 to 0.25
Outputs:
- mixer_out: bfloat16 [8192, 2048], P(('seq', 'exp'))
- expert_mixture: bfloat16 [8192, 2048], P(('seq', 'exp'))
Inputs may be any that keep to these rules, and one draw needn't show every extreme that they name: `route_experts`: each row names 10 different experts. Within the 64 rows of one device (aligned blocks of 64 rows) no expert is named more than 6 times, and in every draw some device names some expert exactly 6 times.
All inputs are finite; a program needn't handle non-finite values.
Results may differ from a plain program's by a relative error of at most 0.02.
Values may be sent and summed in bfloat16 or wider, within the bound.
No kernel may reach another device: no remote copies, remote signals or barrier semaphores. Data moves between devices by JAX's collectives and lax.ppermute only.
A program may use at most 128 MiB of HBM per device.

v0:
```python
import jax
import jax.numpy as jnp
from jax import lax
from jax.sharding import PartitionSpec as P

BLOCK = 64


highest = lax.Precision.HIGHEST
epsilon = 1e-06


def carried_in(shard, axis, join, neutral):
    place = lax.axis_index(axis)
    gathered = jax.tree.map(
        lambda a, kind: lax.all_gather(a.astype(kind), axis), shard, (jnp.bfloat16, jnp.bfloat16)
    )
    state = jax.tree.map(lambda a, e: jnp.zeros_like(a) + jnp.asarray(e, a.dtype), shard, neutral)

    def one(lap, state):
        return join(
            state,
            jax.tree.map(
                lambda a, own: lax.dynamic_index_in_dim(a, lap, 0, False).astype(own.dtype),
                gathered,
                shard,
            ),
        )

    return lax.fori_loop(0, place, one, state)


def shifted(value, axis, steps):
    count = lax.axis_size(axis)
    leading, last = (max(0, -steps), min(count, count - steps))
    return lax.ppermute(value, axis, [(source, source + steps) for source in range(leading, last)])


def causal_conv(value_rows, kernel, leading):
    padded = jnp.concatenate([leading, value_rows], axis=0)
    length = value_rows.shape[0]
    running = jnp.zeros_like(value_rows)
    for offset in range(kernel.shape[0]):
        running = running + kernel[offset] * padded[offset : offset + length]
    return jax.nn.silu(running)


def block_terms(queries, key_rows, value_rows, beta_gate, log_decay):
    block_size = queries.shape[-2]
    cumulative = jnp.cumsum(log_decay, axis=-1)
    spread = cumulative[..., :, None] - cumulative[..., None, :]
    row_index = lax.broadcasted_iota(jnp.int32, (block_size, block_size), 0)
    col_index = lax.broadcasted_iota(jnp.int32, (block_size, block_size), 1)
    lower_mask = row_index >= col_index
    strict = row_index > col_index
    decay_mask = jnp.where(lower_mask, jnp.exp(jnp.where(lower_mask, spread, 0.0)), 0.0)
    key_key = jnp.einsum("...id,...jd->...ij", key_rows, key_rows, precision=highest)
    coupling = jnp.where(strict, beta_gate[..., :, None] * key_key * decay_mask, 0.0)
    identity = jnp.eye(block_size, dtype=jnp.float32)
    growth = jnp.exp(cumulative)
    stacked = jnp.concatenate(
        [beta_gate[..., None] * value_rows, (beta_gate * growth)[..., None] * key_rows], axis=-1
    )
    solved = jax.scipy.linalg.solve_triangular(
        identity + coupling, stacked, lower=True, unit_diagonal=True
    )
    payload_width = value_rows.shape[-1]
    updates = solved[..., :payload_width]
    key_mix = solved[..., payload_width:]
    scores = jnp.einsum("...id,...jd->...ij", queries, key_rows, precision=highest) * decay_mask
    local_out = jnp.einsum("...ij,...jv->...iv", scores, updates, precision=highest)
    lifted = growth[..., None] * queries - jnp.einsum(
        "...ij,...jd->...id", scores, key_mix, precision=highest
    )
    remain = jnp.exp(cumulative[..., -1:] - cumulative)
    key_tail = key_rows * remain[..., None]
    key_dim = key_rows.shape[-1]
    carry_map = jnp.exp(cumulative[..., -1])[..., None, None] * jnp.eye(
        key_dim, dtype=jnp.float32
    ) - jnp.einsum("...ci,...cj->...ij", key_mix, key_tail, precision=highest)
    write_term = jnp.einsum("...cv,...ck->...vk", updates, key_tail, precision=highest)
    return (local_out, lifted, carry_map, write_term)


def compose(earlier, later):
    early_map, early_memory = earlier
    late_map, late_memory = later
    joined_map = jnp.einsum("hij,hjk->hik", early_map, late_map, precision=highest)
    joined_memory = (
        jnp.einsum("hvj,hjk->hvk", early_memory, late_map, precision=highest) + late_memory
    )
    return (joined_map, joined_memory)


def incoming_memory(map_end, local_end, identity, empty):
    prior_map, prior_memory = carried_in((map_end, local_end), "seq", compose, (identity, empty))
    return prior_memory


def step_memory(memory, block_map, block_write):
    return jnp.einsum("hvd,hde->hve", memory, block_map, precision=highest) + block_write


def expert_mlp(arrived, expert_gate, expert_up, expert_down):
    gate_act = jnp.einsum(
        "secd,edf->secf", arrived, expert_gate, preferred_element_type=jnp.float32
    )
    up_act = jnp.einsum("secd,edf->secf", arrived, expert_up, preferred_element_type=jnp.float32)
    inner = (jax.nn.silu(gate_act) * up_act).astype(jnp.bfloat16)
    return jnp.einsum(
        "secf,efd->secd", inner, expert_down, preferred_element_type=jnp.float32
    ).astype(jnp.bfloat16)


def body(
    query_proj,
    key_proj,
    value_proj,
    result_valve_maps,
    beta_logit,
    decay_logit,
    decay_rate,
    conv_query,
    conv_key,
    conv_value,
    norm_gain,
    output_weight,
    residual,
    post_gain,
    route_experts,
    route_weights,
    expert_gate,
    expert_up,
    expert_down,
):
    tok_rows = query_proj.shape[0]
    head_dim = norm_gain.shape[0]
    rim_width = conv_query.shape[0] - 1
    key_cols = query_proj.shape[1]
    value_cols = value_proj.shape[1]
    edge = jnp.concatenate(
        [
            query_proj[tok_rows - rim_width :],
            key_proj[tok_rows - rim_width :],
            value_proj[tok_rows - rim_width :],
        ],
        axis=1,
    )
    leading = shifted(edge, "seq", 1).astype(jnp.float32)
    query_conv = causal_conv(query_proj.astype(jnp.float32), conv_query, leading[:, :key_cols])
    key_conv = causal_conv(
        key_proj.astype(jnp.float32), conv_key, leading[:, key_cols : 2 * key_cols]
    )
    value_conv = causal_conv(value_proj.astype(jnp.float32), conv_value, leading[:, 2 * key_cols :])
    key_heads = key_cols // head_dim
    value_heads = value_cols // head_dim
    key_split = key_conv.reshape(tok_rows, key_heads, head_dim)
    key_unit = key_split * lax.rsqrt(
        jnp.sum(key_split * key_split, axis=-1, keepdims=True) + epsilon
    )
    query_rep = jnp.repeat(query_conv.reshape(tok_rows, key_heads, head_dim), 2, axis=1)
    key_rep = jnp.repeat(key_unit, 2, axis=1)
    value_split = value_conv.reshape(tok_rows, value_heads, head_dim)
    beta_gate = jax.nn.sigmoid(beta_logit)
    log_decay = -decay_rate[None, :] * jax.nn.softplus(decay_logit)
    blocks = tok_rows // BLOCK

    def arrange(array):
        return array.reshape(blocks, BLOCK, value_heads, head_dim).transpose(0, 2, 1, 3)

    def arrange_gate(array):
        return array.reshape(blocks, BLOCK, value_heads).transpose(0, 2, 1)

    local_out, lifted, carry_map, write_term = block_terms(
        arrange(query_rep),
        arrange(key_rep),
        arrange(value_split),
        arrange_gate(beta_gate),
        arrange_gate(log_decay),
    )
    identity = jnp.broadcast_to(
        jnp.eye(head_dim, dtype=jnp.float32), (value_heads, head_dim, head_dim)
    )
    empty = jnp.zeros((value_heads, head_dim, head_dim), jnp.float32)

    def advance_maps(carry, block_item):
        memory, prefix = carry
        block_map, block_write = block_item
        memory = step_memory(memory, block_map, block_write)
        prefix = jnp.einsum("hij,hjk->hik", prefix, block_map, precision=highest)
        return ((memory, prefix), None)

    (local_end, map_end), _ = lax.scan(advance_maps, (empty, identity), (carry_map, write_term))
    prior_memory = incoming_memory(map_end, local_end, identity, empty)

    def advance_again(memory, block_item):
        block_out, block_lift, block_map, block_write = block_item
        result = block_out + jnp.einsum("hcd,hvd->hcv", block_lift, memory, precision=highest)
        memory = step_memory(memory, block_map, block_write)
        return (memory, result)

    _, core = lax.scan(advance_again, prior_memory, (local_out, lifted, carry_map, write_term))
    core = core.transpose(0, 2, 1, 3).reshape(tok_rows, value_heads, head_dim)
    gate_heads = result_valve_maps.astype(jnp.float32).reshape(tok_rows, value_heads, head_dim)
    mean_square = jnp.mean(core * core, axis=-1, keepdims=True)
    normed = (
        (core * lax.rsqrt(mean_square + epsilon) * norm_gain * jax.nn.silu(gate_heads))
        .astype(jnp.bfloat16)
        .reshape(tok_rows, value_cols)
    )
    rows_dev = residual.shape[0]
    model_dim = residual.shape[1]
    mixer = lax.psum_scatter(
        jnp.dot(normed, output_weight, preferred_element_type=jnp.float32).astype(jnp.bfloat16),
        "exp",
        scatter_dimension=0,
        tiled=True,
    ).astype(jnp.float32)
    mixer_out = (residual.astype(jnp.float32) + mixer).astype(jnp.bfloat16)
    mixed = mixer_out.astype(jnp.float32)
    moe_in = (
        mixed * lax.rsqrt(jnp.mean(mixed * mixed, axis=-1, keepdims=True) + epsilon) * post_gain
    ).astype(jnp.bfloat16)
    seq_count = lax.axis_size("seq")
    exp_count = lax.axis_size("exp")
    devices = seq_count * exp_count
    exp_dev = expert_gate.shape[0]
    expert_count = exp_dev * devices
    top_picks = route_experts.shape[1]
    capacity = 2 * ((rows_dev * top_picks + expert_count - 1) // expert_count)
    pick_count = rows_dev * top_picks
    linear_labels = route_experts.reshape(-1)
    expert_ids = jnp.arange(expert_count, dtype=jnp.int32)
    pick_table = (linear_labels[:, None] == expert_ids[None, :]).astype(jnp.bfloat16)
    row_index = lax.broadcasted_iota(jnp.int32, (pick_count, pick_count), 0)
    col_index = lax.broadcasted_iota(jnp.int32, (pick_count, pick_count), 1)
    earlier_picks = (row_index > col_index).astype(jnp.bfloat16)
    ranks = jnp.dot(earlier_picks, pick_table, preferred_element_type=jnp.float32)
    slot_index = jnp.take_along_axis(ranks, linear_labels[:, None], axis=1)[:, 0].astype(jnp.int32)
    position = linear_labels * capacity + slot_index
    source_row = (
        jnp.full((expert_count * capacity,), rows_dev, jnp.int32)
        .at[position]
        .set(jnp.arange(pick_count, dtype=jnp.int32) // top_picks)
    )
    padded_rows = jnp.concatenate([moe_in, jnp.zeros((1, model_dim), jnp.bfloat16)], axis=0)
    outgoing = padded_rows[source_row].reshape(devices, exp_dev, capacity, model_dim)
    finished = expert_mlp(
        lax.all_to_all(outgoing, ("seq", "exp"), split_axis=0, concat_axis=0, tiled=True),
        expert_gate,
        expert_up,
        expert_down,
    )
    returned = lax.all_to_all(finished, ("seq", "exp"), split_axis=0, concat_axis=0, tiled=True)
    flat_back = returned.reshape(expert_count * capacity, model_dim)
    picked = flat_back[position].reshape(rows_dev, top_picks, model_dim)
    shares = route_weights / jnp.sum(route_weights, axis=1, keepdims=True)
    expert_mixture = jnp.sum(picked.astype(jnp.float32) * shares[:, :, None], axis=1).astype(
        jnp.bfloat16
    )
    return (mixer_out, expert_mixture)


def solution(mesh):
    in_specs = (
        P("seq", "exp"),
        P("seq", "exp"),
        P("seq", "exp"),
        P("seq", "exp"),
        P("seq", "exp"),
        P("seq", "exp"),
        P("exp"),
        P(None, "exp"),
        P(None, "exp"),
        P(None, "exp"),
        P(),
        P("exp", None),
        P(("seq", "exp"), None),
        P(),
        P(("seq", "exp"), None),
        P(("seq", "exp"), None),
        P(("seq", "exp"), None, None),
        P(("seq", "exp"), None, None),
        P(("seq", "exp"), None, None),
    )
    out_specs = (P(("seq", "exp"), None), P(("seq", "exp"), None))
    return jax.shard_map(body, mesh=mesh, in_specs=in_specs, out_specs=out_specs, check_vma=False)
```

profile of v0, /device:TPU:1, one launch (start us, length us, event | category | flops | bytes accessed | tf_op | source)
XLA Modules:
  0.0 748.5 jit_solution(14716056276222065683)
XLA Ops:
  9.4 4.9 collective-permute-start
  19.6 1.0 convert_element_type.103
  20.6 1.1 convert_element_type.104
  24.2 2.9 fusion.54
  27.1 158.5 %custom-call.4 = f32[4,8,1,64,64]{3,4,2,1,0:T(8,128)S(1)} custom-call(f32[4,8,1,64,64]{4,3,2,1,0:T(8,128)} %fusion.54), custom_call_target="InvertDiagBlocksLowerTriangular" | custom-call | tf_op jit(solution)/shard_map/jit(_solve_triangular)/vmap(vmap())/triangular_solve | solution.py:64
  186.2 2.0 fusion.35
  188.2 5.1 fusion.73
  193.4 5.4 multiply_subtract_fusion
  198.8 1.9 copy.133
  201.6 20.9 %while.39 = (s32[]{:T(128)}, f32[8,128,128]{1,2,0:T(8,128)}, f32[8,128,128]{1,2,0:T(8,128)}, f32[4,8,128,128]{2,3,1,0:T(8,128)S(1)}, f32[4,8,128,128]{2,3,1,0:T(8,128)}, /*index=5*/s32[]{:T(128)}, s32[]{:T(128)}) while((s32[]{:T(128)}, f32[8,128,128]{1,2,0:T(8,128)}, f32[8,128,128]{1,2,0:T(8,128)}, ...), condition=%wide.region_3.4_spmd.clone, body=%wide.region_2.3_spmd.clone.sunk | while | flops 402915328 | bytes 7865463 | solution.py:193
  201.6 1.1 copy.254
  202.7 2.5 fusion.166
  205.2 1.5 convolution_bitcast_fusion.5
  206.7 1.1 copy.254
  207.8 2.5 fusion.166
  210.4 1.5 convolution_bitcast_fusion.5
  211.9 1.1 copy.254
  213.0 2.5 fusion.166
  215.6 1.5 convolution_bitcast_fusion.5
  217.1 1.1 copy.254
  218.2 2.5 fusion.166
  220.8 1.5 convolution_bitcast_fusion.5
  222.4 1.9 copy.135
  224.4 1.9 copy.136
  227.3 2.1 copy_bitcast_fusion
  229.4 1.8 convolution_multiply_fusion
  231.2 2.2 fusion.74
  233.4 2.2 convolution_subtract_fusion
  235.6 43.5 %all-gather.5.cloned.1.call-done = bf16[256,128,128]{2,1,0:T(8,128)(2,1)} async-done(((bf16[8,128,128]{2,1,0:T(8,128)(2,1)}), bf16[256,128,128]{2,1,0:T(8,128)(2,1)}) %all-gather.5.cloned.1.call-update) | async-done | bytes 8388624 | tf_op jit(solution)/shard_map/all_gather | solution.py:16
  279.2 55.2 %all-gather.7.cloned.1.call-done = bf16[256,128,128]{2,1,0:T(8,128)(2,1)} async-done(((bf16[8,128,128]{2,1,0:T(8,128)(2,1)}), bf16[256,128,128]{2,1,0:T(8,128)(2,1)}) %all-gather.7.cloned.1.call-update) | async-done | bytes 8388624 | tf_op jit(solution)/shard_map/all_gather | solution.py:16
  334.5 2.7 while.37
  334.5 1.0 constant_dynamic-slice_fusion.2
  335.7 1.4 fusion.155
  337.1 16.6 %while.38 = (s32[]{:T(128)}, f32[8,128,128]{1,2,0:T(8,128)S(1)}, f32[4,8,64,128]{3,2,1,0:T(8,128)}, f32[4,8,128,128]{2,3,1,0:T(8,128)S(1)}, f32[4,8,128,128]{2,3...) while((s32[]{:T(128)}, f32[8,128,128]{1,2,0:T(8,128)S(1)}, ...), condition=%wide.region_7.8_spmd, body=%wide.region_6.7_spmd.sunk | while | flops 302186496 | bytes 4458581 | solution.py:202
  337.2 2.4 fusion.161
  339.5 1.7 fusion.160
  341.3 2.4 fusion.161
  343.7 1.7 fusion.160
  345.5 2.4 fusion.161
  347.9 1.7 fusion.160
  349.6 2.3 fusion.161
  352.0 1.7 fusion.160
  353.7 1.6 multiply_reduce_fusion.1
  355.5 1.8 copy.143
  357.7 4.7 convolution_convert_fusion
  363.6 5.4 gather_fusion.2
  369.0 4.1 scatter_custom_fusion
  373.1 89.4 %reduce-scatter.2.cloned.1.call-done = bf16[64,2048]{1,0:T(8,128)(2,1)} async-done(((bf16[256,2048]{1,0:T(8,128)(2,1)}), bf16[64,2048]{1,0:T(8,128)(2,1)}) %reduce-scatter.2.cloned.1.call-update) | async-done | bytes 262160 | tf_op jit(solution)/shard_map/reduce_scatter | solution.py:213
  462.5 1.1 fusion.84
  463.9 7.1 gather_fusion
  470.9 11.0 %reshape.274 = bf16[128,2,6,2048]{3,2,1,0:T(8,128)(2,1)} reshape(bf16[1536,2048]{1,0:T(8,128)(2,1)} %gather_fusion) | data formatting | bytes 12582912 | tf_op jit(solution)/shard_map/reshape | solution.py:247
  481.9 9.6 %copy.149 = bf16[128,2,6,2048]{3,1,2,0:T(2,128)(2,1)S(1)} copy(bf16[128,2,6,2048]{3,2,1,0:T(8,128)(2,1)} %reshape.274) | data formatting | bytes 12582912 | tf_op jit(solution)/shard_map/reshape | solution.py:247
  491.6 85.4 %all_to_all.10 = bf16[128,2,6,2048]{3,1,2,0:T(2,128)(2,1)S(1)} all-to-all(bf16[128,2,6,2048]{3,1,2,0:T(2,128)(2,1)S(1)} %copy.149), channel_id=1, replica_groups=mesh['seq'=32,'exp'=4] {'seq','exp'}, dimensions={0} | all-to-all | bytes 12582912 | tf_op jit(solution)/shard_map/all_to_all | solution.py:249
  577.0 2.6 copy-done.5
  579.6 6.9 fusion.24
  586.6 19.3 %convert_bitcast_fusion = bf16[128,2,6,2048]{3,0,2,1:T(8,128)(2,1)} fusion(bf16[2,512,2048]{2,1,0:T(8,128)(2,1)} %param.43, f32[2,128,6,512]{3,1,2,0:T(8,128)S(1)} %fusion.24, bf16[2,2048,512]{2,1,0:T(8,128)(2,1)} %param.41, bf16[128,2,6,2048]{3,1,2,0:T(2,128)(2,1)} %copy-done.5), kind=kOutput, calls=%fused_computation.35 | convolution fusion | flops 6450315264 | bytes 24117248 | tf_op jit(solution)/shard_map/secf,efd->secd/dot_general | solution.py:110
  605.9 12.7 %copy.152 = bf16[128,2,6,2048]{3,1,2,0:T(2,128)(2,1)} copy(bf16[128,2,6,2048]{3,0,2,1:T(8,128)(2,1)} %convert_bitcast_fusion) | data formatting | bytes 12582912 | tf_op jit(solution)/shard_map/convert_element_type | solution.py:112
  618.7 5.2 all-to-all-start.1
  624.0 76.2 %all-to-all-done.1 = bf16[128,2,6,2048]{3,1,2,0:T(2,128)(2,1)} async-done(((bf16[128,2,6,2048]{3,1,2,0:T(2,128)(2,1)}), bf16[128,2,6,2048]{3,1,2,0:T(2,128)(2,1)}, u32[]{:S(2)}, u32[]{:S(2)}) %all-to-all-start.1) | async-done | bytes 6291488 | tf_op jit(solution)/shard_map/all_to_all | solution.py:254
  700.2 10.4 %copy.153 = bf16[128,2,6,2048]{3,2,1,0:T(8,128)(2,1)} copy(bf16[128,2,6,2048]{3,1,2,0:T(2,128)(2,1)} %all-to-all-done.1) | data formatting | bytes 12582912 | tf_op jit(solution)/shard_map/all_to_all | solution.py:254
  710.6 11.0 %reshape.275 = bf16[1536,2048]{1,0:T(8,128)(2,1)} reshape(bf16[128,2,6,2048]{3,2,1,0:T(8,128)(2,1)} %copy.153) | data formatting | bytes 12582912 | tf_op jit(solution)/shard_map/reshape | solution.py:255
  721.6 9.9 %gather_fusion.1 = bf16[640,2048]{1,0:T(8,128)(2,1)S(1)} fusion(bf16[1536,2048]{1,0:T(8,128)(2,1)} %reshape.275, s32[1024]{0:T(1024)S(1)} %pad_clamp_fusion.1), kind=kCustom, calls=%fused_computation.1 | custom fusion | bytes 5245440 | tf_op jit(solution)/shard_map/gather | solution.py:256
  731.6 3.7 reshape.277
  735.2 6.6 multiply_reduce_fusion
  (118 shorter events, 14.8 us)
Async XLA Ops:
  7.2 220.1 %copy-start = (f32[128]{0:T(128)S(1)}, f32[128]{0:T(128)}, u32[]{:S(2)}) copy-start(f32[128]{0:T(128)} %param.35) | copy-start | bytes 1540
  7.2 272.0 %all-gather.5.cloned.1.call-start = ((), (), s32[]{:S(2)}) async-start(), calls=%async_computation.4 | async-start | bytes 8650752 | tf_op jit(solution)/shard_map/all_gather | solution.py:16
  9.4 12.6 %collective-permute-start = (bf16[3,2048]{1,0:T(4,128)(2,1)S(1)}, bf16[3,2048]{1,0:T(4,128)(2,1)S(1)}, u32[]{:S(2)}, u32[]{:S(2)}) collective-permute-start(bf16[3,2048]{1,0:T(4,128)(2,1)S(1)} %pad_maximum_fusion.3), channel_id=1, source_target_pairs={{0,4},{4,8},{8,12},{12,16},{16,20},{20,24},{24,28},{28,32},{32,36}... | collective-permute-start | bytes 36872 | tf_op jit(solution)/shard_map/ppermute | solution.py:36
  188.2 5.1 copy-start.3
  201.5 24.8 %copy-start.7 = (bf16[256,512]{1,0:T(8,128)(2,1)S(1)}, bf16[256,512]{1,0:T(8,128)(2,1)}, u32[]{:S(2)}) copy-start(bf16[256,512]{1,0:T(8,128)(2,1)} %param.25) | copy-start | bytes 786436
  201.6 25.7 %copy-start.12 = (f32[4,512]{1,0:T(4,128)S(1)}, f32[4,512]{1,0:T(4,128)}, u32[]{:S(2)}) copy-start(f32[4,512]{1,0:T(4,128)} %param.32) | copy-start | bytes 24580
  201.6 3.6 copy-start.2
  206.7 3.6 copy-start.2
  211.9 3.6 copy-start.2
  217.1 3.6 copy-start.2
  224.3 110.1 %all-gather.7.cloned.1.call-start = ((), (), s32[]{:S(2)}) async-start(), calls=%async_computation.5 | async-start | bytes 8650752 | tf_op jit(solution)/shard_map/all_gather | solution.py:16
  226.3 236.2 %reduce-scatter.2.cloned.1.call-start = ((), (), s32[]{:S(2)}) async-start(), calls=%async_computation.3 | async-start | bytes 1310720 | tf_op jit(solution)/shard_map/reduce_scatter | solution.py:213
  227.2 4.0 copy-start.4
  353.7 3.9 copy-start.14
  357.7 4.7 copy-start.11
  362.4 100.1 %copy-start.8 = (bf16[64,2048]{1,0:T(8,128)(2,1)S(1)}, bf16[64,2048]{1,0:T(8,128)(2,1)}, u32[]{:S(2)}) copy-start(bf16[64,2048]{1,0:T(8,128)(2,1)} %param.37) | copy-start | bytes 786436
  363.0 100.7 %copy-start.10 = (f32[2048]{0:T(1024)S(1)}, f32[2048]{0:T(1024)}, u32[]{:S(2)}) copy-start(f32[2048]{0:T(1024)} %param.38) | copy-start | bytes 24580
  463.7 7.3 copy-start.6
  491.6 88.1 %copy-start.13 = (bf16[2,2048,512]{2,1,0:T(8,128)(2,1)S(1)}, bf16[2,2048,512]{2,1,0:T(8,128)(2,1)}, u32[]{:S(2)}) copy-start(bf16[2,2048,512]{2,1,0:T(8,128)(2,1)} %param.42) | copy-start | bytes 12582916
  577.0 2.6 copy-start.5
  618.6 5.2 copy-start.9
  618.7 81.5 %all-to-all-start.1 = ((bf16[128,2,6,2048]{3,1,2,0:T(2,128)(2,1)}), bf16[128,2,6,2048]{3,1,2,0:T(2,128)(2,1)}, u32[]{:S(2)}, u32[]{:S(2)}) async-start(bf16[128,2,6,2048]{3,1,2,0:T(2,128)(2,1)} %copy.152), calls=%async_computation.2 | async-start | bytes 12582912 | tf_op jit(solution)/shard_map/all_to_all | solution.py:254
  731.5 10.3 %copy-start.1 = (f32[128]{0:T(128)S(1)}, f32[128]{0:T(128)}, u32[]{:S(2)}) copy-start(f32[128]{0:T(128)} %param.35) | copy-start | bytes 1540
Sparse Core Ops, SparseCore 0:
  224.5 54.6 all-gather.4
  282.0 52.3 all-gather.6
  362.5 99.9 reduce-scatter.1
where the time goes:
time: 756 us; the launch traced here: 749 us
  waiting for transfers between devices  264 us (35%)
  other arithmetic  179 us (24%)
  local copies, waits for them, and re-layouts  108 us (14%)
  matrix products  87 us (12%)
  blocking collectives  85.4 us (11%)
  between operations  14.5 us (2%)
  starting transfers between devices  10.2 us (1%)
    another operation x4, other arithmetic, block_terms(): jax.scipy.linalg.solve_triangular(identity + coupling, stacked, lower=Tru...  159 us
    all_gather x2, waiting for transfers between devices, carried_in(): lax.all_gather(a.astype(kind), axis)  98.8 us
    reduce_scatter x1, waiting for transfers between devices, body(): lax.psum_scatter(jnp.dot(normed, output_weight, preferred_element_type=jn...  89.4 us
    all_to_all x1, blocking collectives, body(): lax.all_to_all(outgoing, ('seq', 'exp'), split_axis=0, concat_axis=0, til...  85.4 us
    all_to_all x1, waiting for transfers between devices, body(): lax.all_to_all(finished, ('seq', 'exp'), split_axis=0, concat_axis=0, til...  76.2 us
    reshape x2, local copies, waits for them, and re-layouts, body(): padded_rows[source_row].reshape(devices, exp_dev, capacity, model_dim)  20.6 us
    dot_general x1, matrix products, expert_mlp(): jnp.einsum('secf,efd->secd', inner, expert_down, preferred_element_type=j...  19.3 us
    dot_general x8, matrix products, step_memory(): jnp.einsum('hvd,hde->hve', memory, block_map, precision=highest)  17 us
  transfers between devices with their start and end apart: 5, of which 4 were waited for; matrix products, arithmetic and copies ran while one was open for 4% of the time, Pallas kernels for 0%

commit v1 on v0

v1 whole, which is shorter than its diff:
```python
import jax
import jax.numpy as jnp
from jax import lax
from jax.experimental import pallas as pl
from jax.experimental.pallas import tpu as pltpu
from jax.sharding import PartitionSpec as P

f32 = jnp.float32
bf16 = jnp.bfloat16
EPS = 1e-06
HD = 128
BLK = 128
TOK = 256
HALO = 8
SEQ = 32
NEAR = 8
FAR = SEQ // NEAR
EXP = 4
DEV = SEQ * EXP
ROWS = 64
PICKS = 10
CAP = 6
NQ = 4
CH = 2 * CAP * NQ
QW = 512
FF = 512
VMEM = 56 * 1024 * 1024


def iota(shape, dim):
    return lax.broadcasted_iota(jnp.int32, shape, dim)


def split(a):
    hi = a.astype(bf16)
    return hi, (a - hi.astype(f32)).astype(bf16)


def dot(a, b, dims=((1,), (0,))):
    return lax.dot_general(a, b, (dims, ((), ())), preferred_element_type=f32)


def dot3(a, b, dims=((1,), (0,))):
    return dot(a[0], b[0], dims) + (dot(a[0], b[1], dims) + dot(a[1], b[0], dims))


NT = ((1,), (1,))
TN = ((0,), (0,))


def conv_silu(ref, halo_ref, taps_ref, pad_ref):
    width = ref.shape[1]
    pad_ref[0:HALO, 0:width] = halo_ref[...].astype(f32)
    pad_ref[HALO : HALO + TOK, 0:width] = ref[...].astype(f32)
    run = taps_ref[0:1, :] * pad_ref[HALO - 3 : HALO - 3 + TOK, 0:width]
    for j in range(1, 4):
        run = run + taps_ref[j : j + 1, :] * pad_ref[HALO - 3 + j : HALO - 3 + j + TOK, 0:width]
    return run / (1.0 + jnp.exp(-run))


def odd_rows(x, size):
    return jnp.concatenate(
        [x[m * size : (m + 1) * size] for m in range(1, BLK // size, 2)], axis=0
    )


def inverses(couplings):
    count = len(couplings)
    lane = iota((8, BLK), 1)
    sub = iota((8, BLK), 0)
    slabs = [[] for _ in range(count)]
    for m in range(BLK // 8):
        a = [c[8 * m : 8 * m + 8] for c in couplings]
        t = [(lane == sub + 8 * m).astype(f32)] * count
        for j in range(7):
            t = [t[n] - a[n][:, 8 * m + j : 8 * m + j + 1] * t[n][j : j + 1, :] for n in range(count)]
        for n in range(count):
            slabs[n].append(t[n])
    ts = [jnp.concatenate(x, axis=0) for x in slabs]
    half = BLK // 2
    rows = iota((half, BLK), 0)
    cols = iota((half, BLK), 1)
    size = 8
    while size < BLK:
        part = cols // size == 2 * (rows // size)
        zero = jnp.zeros((size, BLK), f32)
        prods = [
            dot3(split(jnp.where(part, odd_rows(c, size), 0.0)), split(t)) for c, t in zip(couplings, ts)
        ]
        lowers = []
        for prod, t in zip(prods, ts):
            tall = []
            for m in range(half // size):
                tall += [zero, prod[m * size : (m + 1) * size]]
            lower = odd_rows(t, size)
            lowers.append(lower - dot3(split(lower), split(jnp.concatenate(tall, axis=0))))
        new = []
        for lower, t in zip(lowers, ts):
            pieces = []
            for m in range(half // size):
                pieces += [t[2 * m * size : (2 * m + 1) * size], lower[m * size : (m + 1) * size]]
            new.append(jnp.concatenate(pieces, axis=0))
        ts = new
        size *= 2
    return [split(t) for t in ts]


def mixer_body(q_ref, k_ref, v_ref, hq_ref, hk_ref, hv_ref, bl_ref, dl_ref, rate_ref, cq_ref, ck_ref, cv_ref,
               map_ref, local_ref, lift_ref, pad_ref, cum_ref, beta_ref):
    step = pl.program_id(0)
    row = iota((BLK, BLK), 0)
    col = iota((BLK, BLK), 1)
    x = dl_ref[...]
    soft = jnp.maximum(x, 0.0) + jnp.log1p(jnp.exp(-jnp.abs(x)))
    decay = jnp.maximum(-rate_ref[...] * soft, -110.0)
    upper = (row <= col).astype(f32)
    for b in range(2):
        cum_ref[b] = lax.dot_general(decay[:, b * BLK : (b + 1) * BLK], upper, (((1,), (0,)), ((), ())),
                                     precision=lax.Precision.HIGHEST, preferred_element_type=f32)
        beta_ref[b] = 1.0 / (1.0 + jnp.exp(-bl_ref[:, b * BLK : (b + 1) * BLK]))

    queries = conv_silu(q_ref, hq_ref, cq_ref, pad_ref)
    keys = conv_silu(k_ref, hk_ref, ck_ref, pad_ref)
    keys = keys * lax.rsqrt(jnp.sum(keys * keys, axis=1, keepdims=True) + EPS)
    values = conv_silu(v_ref, hv_ref, cv_ref, pad_ref)

    rows = []
    for b in range(2):
        for i in range(2):
            rows.append(cum_ref[b, pl.ds(2 * step + i, 1), :])
            rows.append(beta_ref[b, pl.ds(2 * step + i, 1), :])
    wide = jnp.concatenate(rows + [jnp.zeros((BLK - 8, BLK), f32)], axis=0)
    tall = wide.T

    res = {}
    keyed = [(b, i) for b in range(2) for i in range(2)]
    grams, scores, masks, couplings = {}, {}, {}, []
    for b in range(2):
        kb = split(keys[b * BLK : (b + 1) * BLK])
        grams[b] = dot3(kb, kb, NT)
        scores[b] = dot(queries[b * BLK : (b + 1) * BLK].astype(bf16), kb[0], NT)
    for b, i in keyed:
        at = 2 * (2 * b + i)
        spread = tall[:, at : at + 1] - rows[at]
        masks[b, i] = jnp.where(row >= col, jnp.exp(jnp.where(row >= col, spread, 0.0)), 0.0)
        couplings.append(jnp.where(row > col, tall[:, at + 1 : at + 2] * grams[b] * masks[b, i], 0.0))
    invs = dict(zip(keyed, inverses(couplings)))
    for b, i in keyed:
        at = 2 * (2 * b + i)
        cum_c = tall[:, at : at + 1]
        beta_c = tall[:, at + 1 : at + 2]
        qb = queries[b * BLK : (b + 1) * BLK]
        kb = keys[b * BLK : (b + 1) * BLK]
        vb = values[b * BLK : (b + 1) * BLK, i * HD : (i + 1) * HD]
        grow = jnp.exp(cum_c)
        last = cum_c[BLK - 1 : BLK, :]
        key_tail = (kb * jnp.exp(last - cum_c)).astype(bf16)
        rhs = jnp.concatenate([beta_c * vb, (beta_c * grow) * kb], axis=1)
        solved = dot3(invs[b, i], split(rhs)).astype(bf16)
        near = dot((scores[b] * masks[b, i]).astype(bf16), solved)
        local = near[:, :HD]
        lift = grow * qb - near[:, HD:]
        both = dot(solved, key_tail, TN)
        res[b, i] = (local, lift, jnp.exp(last), both)
    for i in range(2):
        l0, f0, t0, both0 = res[0, i]
        l1, f1, t1, both1 = res[1, i]
        w0, gone0 = both0[:HD], both0[HD:]
        w1, gone1 = both1[:HD], both1[HD:]
        first = both0.astype(bf16)
        joined = dot(first, gone1.astype(bf16))
        w = t1 * w0 - joined[:HD] + w1
        m = (t0 * t1) * (row == col).astype(f32) - t0 * gone1 - t1 * gone0 + joined[HD:]
        moved = dot(f1.astype(bf16), first, NT)
        local_ref[i, 0:BLK] = l0
        local_ref[i, BLK:TOK] = l1 + moved[:, :HD]
        lift_ref[i, 0:BLK] = f0.astype(bf16)
        lift_ref[i, BLK:TOK] = (t0 * f1 - moved[:, HD:]).astype(bf16)
        map_ref[i, 0:HD] = m.astype(bf16)
        map_ref[i, HD : 2 * HD] = w.astype(bf16)


def mixer_blocks(q, k, v, halo, beta_t, decay_t, rate, cq, ck, cv):
    w = HD
    return pl.pallas_call(
        mixer_body,
        grid=(4,),
        in_specs=[
            pl.BlockSpec((TOK, w), lambda s: (0, s)),
            pl.BlockSpec((TOK, w), lambda s: (0, s)),
            pl.BlockSpec((TOK, 2 * w), lambda s: (0, s)),
            pl.BlockSpec((HALO, w), lambda s: (0, s)),
            pl.BlockSpec((HALO, w), lambda s: (0, 4 + s)),
            pl.BlockSpec((HALO, 2 * w), lambda s: (0, 4 + s)),
            pl.BlockSpec((8, TOK), lambda s: (0, 0)),
            pl.BlockSpec((8, TOK), lambda s: (0, 0)),
            pl.BlockSpec((8, 1), lambda s: (0, 0)),
            pl.BlockSpec((4, w), lambda s: (0, s)),
            pl.BlockSpec((4, w), lambda s: (0, s)),
            pl.BlockSpec((4, 2 * w), lambda s: (0, s)),
        ],
        out_specs=[
            pl.BlockSpec((2, 2 * HD, HD), lambda s: (s, 0, 0)),
            pl.BlockSpec((2, TOK, HD), lambda s: (s, 0, 0)),
            pl.BlockSpec((2, TOK, HD), lambda s: (s, 0, 0)),
        ],
        out_shape=[
            jax.ShapeDtypeStruct((NEAR, 2 * HD, HD), bf16),
            jax.ShapeDtypeStruct((8, TOK, HD), f32),
            jax.ShapeDtypeStruct((8, TOK, HD), bf16),
        ],
        scratch_shapes=[
            pltpu.VMEM((TOK + HALO, 2 * HD), f32),
            pltpu.VMEM((2, 8, BLK), f32),
            pltpu.VMEM((2, 8, BLK), f32),
        ],
        compiler_params=pltpu.CompilerParams(vmem_limit_bytes=VMEM),
        name="mixer_blocks",
    )(q, k, v, halo, halo, halo, beta_t, decay_t, rate, cq, ck, cv)


def in_vmem(count):
    return [pl.BlockSpec(memory_space=pltpu.VMEM)] * count


def vmem(mib):
    return pltpu.CompilerParams(vmem_limit_bytes=mib * 1024 * 1024)


def near_body(in_ref, map_ref, mem_ref, all_ref):
    both = in_ref[0].astype(f32)
    for j in range(1, NEAR):
        hi, lo = split(both)
        map_ref[j - 1] = hi[:HD]
        mem_ref[j - 1] = both[HD:]
        here = in_ref[j]
        both = dot(hi, here[:HD]) + dot(lo, here[:HD])
        both = jnp.concatenate([both[:HD], both[HD:] + here[HD:].astype(f32)], axis=0)
    for g in range(FAR):
        all_ref[g] = both.astype(bf16)


def near_scan(maps):
    return pl.pallas_call(
        near_body,
        in_specs=in_vmem(1),
        out_shape=[
            jax.ShapeDtypeStruct((NEAR - 1, HD, HD), bf16),
            jax.ShapeDtypeStruct((NEAR - 1, HD, HD), f32),
            jax.ShapeDtypeStruct((FAR, 2 * HD, HD), bf16),
        ],
        compiler_params=vmem(8),
        name="near_scan",
    )(maps)


def far_body(at_ref, all_ref, map_ref, mem_ref, out_ref):
    state = jnp.zeros((HD, HD), f32)
    entry = state
    for g in range(FAR - 1):
        if g == 0:
            state = all_ref[0, HD:].astype(f32)
        else:
            hi, lo = split(state)
            here = all_ref[g]
            state = dot(hi, here[:HD]) + dot(lo, here[:HD]) + here[HD:].astype(f32)
        entry = jnp.where(at_ref[0] == g + 1, state, entry)
    hi, lo = split(entry)
    out_ref[0] = hi
    for j in range(1, NEAR):
        m = map_ref[j - 1]
        out_ref[j] = (dot(hi, m) + dot(lo, m) + mem_ref[j - 1]).astype(bf16)


def far_scan(place, totals, maps, memories):
    return pl.pallas_call(
        far_body,
        in_specs=[pl.BlockSpec(memory_space=pltpu.SMEM)] + in_vmem(3),
        out_shape=jax.ShapeDtypeStruct((NEAR, HD, HD), bf16),
        compiler_params=vmem(8),
        name="far_scan",
    )(place, totals, maps, memories)


def project_body(s_ref, local_ref, lift_ref, gate_ref, gain_ref, w_ref, out_ref, norm_ref):
    for h in range(8):
        core = local_ref[h] + dot(lift_ref[h], s_ref[h], NT)
        gate = gate_ref[:, h * HD : (h + 1) * HD].astype(f32)
        ms = jnp.sum(core * core, axis=1, keepdims=True) * (1.0 / HD)
        act = gate / (1.0 + jnp.exp(-gate))
        norm_ref[:, h * HD : (h + 1) * HD] = (core * lax.rsqrt(ms + EPS) * gain_ref[...] * act).astype(bf16)
    for n in range(4):
        out = dot(norm_ref[...], w_ref[:, n * QW : (n + 1) * QW]).astype(bf16)
        for e in range(EXP):
            out_ref[e, :, n * QW : (n + 1) * QW] = out[e * ROWS : (e + 1) * ROWS]


def project(states, local, lift, gate, gain, weight):
    return pl.pallas_call(
        project_body,
        in_specs=in_vmem(6),
        out_shape=jax.ShapeDtypeStruct((EXP, ROWS, 2048), bf16),
        scratch_shapes=[pltpu.VMEM((TOK, 8 * HD), bf16)],
        compiler_params=vmem(16),
        name="project",
    )(states, local, lift, gate, gain, weight)


def route_body(experts_ref, weights_ref, pick_ref, part_ref, slot_ref, share_ref):
    ids = experts_ref[...]
    weights = weights_ref[...]
    shares = weights / jnp.sum(weights, axis=1, keepdims=True)
    lane = iota((ROWS, DEV), 1)
    token = iota((ROWS, DEV), 0).astype(f32)
    earlier = (iota((ROWS, ROWS), 0) > iota((ROWS, ROWS), 1)).astype(bf16)
    for e in range(2):
        named = jnp.zeros((ROWS, DEV), f32)
        part = jnp.zeros((ROWS, DEV), f32)
        for k in range(PICKS):
            hit = ids[:, k : k + 1] == 2 * lane + e
            named = named + jnp.where(hit, 1.0, 0.0)
            part = part + jnp.where(hit, shares[:, k : k + 1], 0.0)
        rank = dot(earlier, named.astype(bf16))
        for r in range(CAP):
            hit = (named > 0.5) & (rank == float(r))
            used = jnp.sum(jnp.where(hit, 1.0, 0.0), axis=0, keepdims=True)
            tok = jnp.sum(jnp.where(hit, token, 0.0), axis=0, keepdims=True)
            share = jnp.sum(jnp.where(hit, part, 0.0), axis=0, keepdims=True)
            for q in range(NQ):
                j = q * 2 * CAP + e * CAP + r
                slot_ref[j : j + 1, :] = jnp.where(used > 0.5, tok + float(ROWS * q), -1.0)
                share_ref[j : j + 1, :] = share
    slots = slot_ref[...]
    shs = share_ref[...]
    lane2 = iota((CH, NQ * ROWS), 1).astype(f32)
    for g in range(DEV // 8):
        tall = []
        for d in range(8 * g, 8 * g + 8):
            hit = slots[:, d : d + 1] == lane2
            pick_ref[d * CH : (d + 1) * CH, :] = jnp.where(hit, 1.0, 0.0).astype(bf16)
            tall.append(jnp.where(hit, shs[:, d : d + 1], 0.0))
        part_ref[:, g * 8 * CH : (g + 1) * 8 * CH] = jnp.concatenate(tall, axis=0).T.astype(bf16)


def route(experts, weights):
    return pl.pallas_call(
        route_body,
        out_shape=[
            jax.ShapeDtypeStruct((DEV * CH, NQ * ROWS), bf16),
            jax.ShapeDtypeStruct((NQ * ROWS, DEV * CH), bf16),
        ],
        scratch_shapes=[pltpu.VMEM((CH, DEV), f32), pltpu.VMEM((CH, DEV), f32)],
        compiler_params=vmem(16),
        name="route",
    )(experts, weights)


def dispatch_body(parts_ref, res_ref, gain_ref, pick_ref, mix_ref, out_ref, stack_ref):
    total = parts_ref[0].astype(f32)
    for e in range(1, EXP):
        total = total + parts_ref[e].astype(f32)
    mixed = (res_ref[...].astype(f32) + total).astype(bf16)
    mix_ref[...] = mixed
    m = mixed.astype(f32)
    ms = jnp.sum(m * m, axis=1, keepdims=True) * (1.0 / (NQ * QW))
    normed = (m * lax.rsqrt(ms + EPS) * gain_ref[...]).astype(bf16)
    for q in range(NQ):
        stack_ref[q * ROWS : (q + 1) * ROWS, :] = normed[:, q * QW : (q + 1) * QW]
    step = DEV * CH // 8
    for n in range(8):
        out_ref[n * step : (n + 1) * step, :] = dot(
            pick_ref[n * step : (n + 1) * step, :], stack_ref[...]
        ).astype(bf16)


def dispatch(parts, residual, gain, pick):
    return pl.pallas_call(
        dispatch_body,
        in_specs=in_vmem(4),
        out_shape=[
            jax.ShapeDtypeStruct((ROWS, 2048), bf16),
            jax.ShapeDtypeStruct((DEV * CH, QW), bf16),
        ],
        scratch_shapes=[pltpu.VMEM((NQ * ROWS, QW), bf16)],
        compiler_params=vmem(16),
        name="dispatch",
    )(parts, residual, gain, pick)


GS = 4
GR = GS * CH
PR = GS * CAP


def expert_body(in_ref, gate_ref, up_ref, down_ref, out_ref, x_ref, y_ref):
    def place(n):
        rest = n % CH
        return (rest // CAP) * PR + (n // CH) * CAP + rest % CAP

    perm = (iota((GR, GR), 0) == place(iota((GR, GR), 1))).astype(bf16)
    perm_t = (iota((GR, GR), 1) == place(iota((GR, GR), 0))).astype(bf16)
    pairs = DEV // (2 * GS)

    def load(i, _):
        a = dot(perm, in_ref[pl.ds(2 * GR * i, GR), :])
        b = dot(perm, in_ref[pl.ds(2 * GR * i + GR, GR), :])
        for q in range(NQ):
            for e in range(2):
                at = (2 * q + e) * PR
                both = jnp.concatenate([a[at : at + PR], b[at : at + PR]], axis=0).astype(bf16)
                x_ref[e, pl.ds(2 * PR * i, 2 * PR), q * QW : (q + 1) * QW] = both
        return 0

    lax.fori_loop(0, pairs, load, 0, unroll=2)
    for e in range(2):
        x = x_ref[e]
        g = dot(x, gate_ref[e])
        u = dot(x, up_ref[e])
        inner = (g / (1.0 + jnp.exp(-g)) * u).astype(bf16)
        y_ref[e] = dot(inner, down_ref[e]).astype(bf16)

    def store(i, _):
        halves = ([], [])
        for q in range(NQ):
            for e in range(2):
                both = y_ref[e, pl.ds(2 * PR * i, 2 * PR), q * QW : (q + 1) * QW].astype(f32)
                halves[0].append(both[:PR])
                halves[1].append(both[PR:])
        for h in range(2):
            z = jnp.concatenate(halves[h], axis=0).astype(bf16)
            out_ref[pl.ds(2 * GR * i + GR * h, GR), :] = dot(perm_t, z).astype(bf16)
        return 0

    lax.fori_loop(0, pairs, store, 0, unroll=2)


def experts_mlp(arrived, gate, up, down):
    return pl.pallas_call(
        expert_body,
        in_specs=in_vmem(4),
        out_shape=jax.ShapeDtypeStruct((DEV * CH, QW), bf16),
        scratch_shapes=[
            pltpu.VMEM((2, DEV * CAP, 2048), bf16),
            pltpu.VMEM((2, DEV * CAP, 2048), bf16),
        ],
        compiler_params=vmem(26),
        name="experts_mlp",
    )(arrived, gate, up, down)


def combine_body(part_ref, back_ref, out_ref):
    acc = dot(part_ref[...], back_ref[...])
    for q in range(NQ):
        out_ref[:, q * QW : (q + 1) * QW] = acc[q * ROWS : (q + 1) * ROWS, :].astype(bf16)


def combine(part, back):
    return pl.pallas_call(
        combine_body,
        in_specs=in_vmem(2),
        out_shape=jax.ShapeDtypeStruct((ROWS, 2048), bf16),
        compiler_params=vmem(8),
        name="combine",
    )(part, back)


def exchange(rows):
    chunks = rows.reshape(DEV, CH, QW)
    moved = lax.all_to_all(chunks, ("seq", "exp"), split_axis=0, concat_axis=0, tiled=True)
    return moved.reshape(DEV * CH, QW)


def body(
    query_proj,
    key_proj,
    value_proj,
    result_valve_maps,
    beta_logit,
    decay_logit,
    decay_rate,
    conv_query,
    conv_key,
    conv_value,
    norm_gain,
    output_weight,
    residual,
    post_gain,
    route_experts,
    route_weights,
    expert_gate,
    expert_up,
    expert_down,
):
    edge = jnp.concatenate(
        [a[TOK - HALO :] for a in (query_proj, key_proj, value_proj)], axis=1
    )
    halo = lax.ppermute(edge, "seq", [(s, s + 1) for s in range(SEQ - 1)])
    pick, share = route(route_experts, route_weights)
    maps, local, lift = mixer_blocks(
        query_proj,
        key_proj,
        value_proj,
        halo,
        beta_logit.T,
        decay_logit.T,
        decay_rate[:, None],
        conv_query,
        conv_key,
        conv_value,
    )
    near = [[g * NEAR + j for j in range(NEAR)] for g in range(FAR)]
    far = [[g * NEAR + j for g in range(FAR)] for j in range(NEAR)]

    def swap(array, groups):
        return lax.all_to_all(array, "seq", split_axis=0, concat_axis=0, axis_index_groups=groups, tiled=True)

    before, memories, totals = near_scan(swap(maps, near))
    place = (lax.axis_index("seq") // NEAR).astype(jnp.int32).reshape(1)
    states = swap(far_scan(place, swap(totals, far), before, memories), near)
    parts = project(
        states, local, lift, result_valve_maps, norm_gain[None, :], output_weight
    )
    parts = lax.all_to_all(parts, "exp", split_axis=0, concat_axis=0, tiled=True)
    mixer_out, outgoing = dispatch(parts, residual, post_gain[None, :], pick)
    finished = experts_mlp(exchange(outgoing), expert_gate, expert_up, expert_down)
    return (mixer_out, combine(share, exchange(finished)))


def solution(mesh):
    wide = P("seq", "exp")
    rows = P(("seq", "exp"), None)
    whole = P(("seq", "exp"), None, None)
    taps = P(None, "exp")
    in_specs = (wide, wide, wide, wide, wide, wide, P("exp"), taps, taps, taps, P(), P("exp", None), rows, P(), rows, rows, whole, whole, whole)
    return jax.shard_map(body, mesh=mesh, in_specs=in_specs, out_specs=(rows, rows), check_vma=False)
```

time: 756 us -> 274 us (0.36)
  waiting for transfers between devices: 264 us -> 13 us
  other arithmetic: 179 us -> 0.01 us
  blocking collectives: 85.4 us -> 187 us
  local copies, waits for them, and re-layouts: 108 us -> 11.7 us
  matrix products: 87 us -> 0 us
  Pallas kernels: 0 us -> 47.2 us
  between operations: 14.5 us -> 0.79 us
    another operation x5 -> x0, other arithmetic: 159 us -> none  [the longest x4 159 us: block_terms(): jax.scipy.linalg.solve_triangular(identity + coupling, stacked, lower=Tru...]
    all_to_all x1 -> x4, blocking collectives: 85.4 us -> 187 us  [the longest x2 161 us: exchange(): lax.all_to_all(chunks, ('seq', 'exp'), split_axis=0, concat_axis=0, tiled...]
    all_gather x2 -> x0, waiting for transfers between devices: 98.8 us -> none  [carried_in(): lax.all_gather(a.astype(kind), axis)]
    reduce_scatter x1 -> x0, waiting for transfers between devices: 89.4 us -> none  [body(): lax.psum_scatter(jnp.dot(normed, output_weight, preferred_element_type=jn...]
    dot_general x27 -> x0, matrix products: 85 us -> none  [the longest x1 19.3 us: expert_mlp(): jnp.einsum('secf,efd->secd', inner, expert_down, preferred_element_type=j...]
    all_to_all x1 -> x2, waiting for transfers between devices: 76.2 us -> 13 us  [the longest x1 7.46 us: body(): lax.all_to_all(parts, 'exp', split_axis=0, concat_axis=0, tiled=True)]
    pallas_call x0 -> x8, Pallas kernels: none -> 47.2 us  [the longest x1 18.5 us: mixer_blocks(): pl.pallas_call(mixer_body, grid=(4,), in_specs=[pl.BlockSpec((TOK, w), la...]
    reshape x9 -> x0, local copies, waits for them, and re-layouts: 32.1 us -> none  [the longest x2 20.6 us: body(): padded_rows[source_row].reshape(devices, exp_dev, capacity, model_dim)]
  transfers between devices with their start and end apart: 5 -> 3, of which waited for: 4 -> 2; matrix products, arithmetic and copies ran while one was open for 4% -> 1% of each run, Pallas kernels for 0% -> 1%
where the time goes in v1:
time: 274 us; the launch traced here: 273 us
  blocking collectives  187 us (68%)
  Pallas kernels  47.2 us (17%)
  starting transfers between devices  13.3 us (5%)
  waiting for transfers between devices  13 us (5%)
  local copies, waits for them, and re-layouts  11.7 us (4%)
    all_to_all x2, blocking collectives, exchange(): lax.all_to_all(chunks, ('seq', 'exp'), split_axis=0, concat_axis=0, tiled...  161 us
    all_to_all x2, blocking collectives, swap(): lax.all_to_all(array, 'seq', split_axis=0, concat_axis=0, axis_index_grou...  26.6 us
    pallas_call x1, Pallas kernels, mixer_blocks(): pl.pallas_call(mixer_body, grid=(4,), in_specs=[pl.BlockSpec((TOK, w), la...  18.5 us
    pallas_call x1, Pallas kernels, experts_mlp(): pl.pallas_call(expert_body, in_specs=in_vmem(4), out_shape=jax.ShapeDtype...  15.9 us
    unnamed x36, local copies, waits for them, and re-layouts  8.22 us
    all_to_all x1, waiting for transfers between devices, body(): lax.all_to_all(parts, 'exp', split_axis=0, concat_axis=0, tiled=True)  7.46 us
    all_to_all x1, waiting for transfers between devices, swap(): lax.all_to_all(array, 'seq', split_axis=0, concat_axis=0, axis_index_grou...  5.53 us
  transfers between devices with their start and end apart: 3, of which 2 were waited for; matrix products, arithmetic and copies ran while one was open for 1% of the time, Pallas kernels for 1%

profile of v1, /device:TPU:1, one launch (start us, length us, event | category | flops | bytes accessed | tf_op | source)
XLA Modules:
  0.0 273.1 jit_solution(10552313387585354134)
XLA Ops:
  0.6 0.0 copy-start.13
  0.6 0.0 copy-start.9
  0.6 0.8 slice.9
  1.4 0.7 slice.10
  2.1 0.7 slice.11
  2.8 4.9 %collective-permute-start = (bf16[8,2048]{1,0:T(8,128)(2,1)S(1)}, bf16[8,2048]{1,0:T(8,128)(2,1)S(1)}, u32[]{:S(2)}, u32[]{:S(2)}) collective-permute-start(bf16[8,2048]{1,0:T(8,128)(2,1)S(1)} %pad_maximum_fusion), channel_id=1, source_target_pairs={{0,4},{4,8},{8,12},{12,16},{16,20},{20,24},{24,28},{28,32},{32,36}... | collective-permute-start | bytes 98312 | tf_op jit(solution)/shard_map/ppermute | solution.py:497
  7.8 1.3 copy.21.rate_ref
  9.1 0.0 collective-permute-done.hq_ref.hk_ref.hv_ref
  9.1 0.0 copy-start.14
  9.1 0.6 copy-done.14
  9.7 18.5 %mixer_blocks.1 = (bf16[8,256,128]{2,1,0:T(8,128)(2,1)}, f32[8,256,128]{2,1,0:T(8,128)}, bf16[8,256,128]{2,1,0:T(8,128)(2,1)}) custom-call(bf16[256,512]{1,0:T(8,128)(2,1)} %q_ref.1, bf16[256,512]{1,0:T(8,128)(2,1)} %k_ref.1, bf16[256,1024]{1,0:T(8,128)(2,1)} %v_ref.1, bf16[8,2048]{1,0:T(8,128)(2,1)} %copy-done.14, bf16[8,2048]{1,0:T(8,128)(2,1)} %copy-done.14, ...), custom_call_target="tpu_custom_call" | custom-call | tf_op jit(solution)/shard_map/mixer_blocks/pallas_call | solution.py:185
  28.2 0.0 copy-start.8
  28.2 0.0 copy-start.10
  28.2 15.2 %all_to_all.30.in_ref = bf16[8,256,128]{2,1,0:T(8,128)(2,1)S(1)} all-to-all(bf16[8,256,128]{2,1,0:T(8,128)(2,1)} %get-tuple-element.12), channel_id=1, replica_groups={{0,4,8,12,16,20,24,28},{32,36,40,44,48,52,56,60},{64,68,72,76,80,84,88,..., dimensions={0} | all-to-all | bytes 1048576 | tf_op jit(solution)/shard_map/all_to_all | solution.py:515
  43.5 1.8 near_scan.1
  45.3 4.4 %all-to-all-start.1 = ((bf16[4,256,128]{2,1,0:T(8,128)(2,1)}), bf16[4,256,128]{2,1,0:T(8,128)(2,1)S(1)}, u32[]{:S(2)}, u32[]{:S(2)}) async-start(bf16[4,256,128]{2,1,0:T(8,128)(2,1)} %get-tuple-element.13), calls=%async_computation.1 | async-start | bytes 524288 | tf_op jit(solution)/shard_map/all_to_all | solution.py:515
  49.7 5.5 %all-to-all-done.1.all_ref = bf16[4,256,128]{2,1,0:T(8,128)(2,1)S(1)} async-done(((bf16[4,256,128]{2,1,0:T(8,128)(2,1)}), bf16[4,256,128]{2,1,0:T(8,128)(2,1)S(1)}, u32[]{:S(2)}, u32[]{:S(2)}) %all-to-all-start.1) | async-done | bytes 262176 | tf_op jit(solution)/shard_map/all_to_all | solution.py:515
  55.2 0.6 far_scan.1
  55.8 11.3 %all_to_all.31.s_ref = bf16[8,128,128]{2,1,0:T(8,128)(2,1)S(1)} all-to-all(bf16[8,128,128]{2,1,0:T(8,128)(2,1)S(1)} %far_scan.1), channel_id=1, replica_groups={{0,4,8,12,16,20,24,28},{32,36,40,44,48,52,56,60},{64,68,72,76,80,84,88,..., dimensions={0} | all-to-all | bytes 524288 | tf_op jit(solution)/shard_map/all_to_all | solution.py:515
  67.1 0.0 copy-done.13
  67.1 0.0 copy-done.9
  67.1 0.0 copy-done.8
  67.1 0.0 copy-done.10
  67.1 0.0 copy-start
  67.2 2.2 copy-done
  69.3 0.0 copy-start.15
  69.3 0.0 copy-start.16
  69.3 0.0 copy-start.11
  69.3 0.0 copy-start.12
  69.3 2.8 %project.1 = bf16[4,64,2048]{2,1,0:T(8,128)(2,1)} custom-call(bf16[8,128,128]{2,1,0:T(8,128)(2,1)S(1)} %all_to_all.31.s_ref, f32[8,256,128]{2,1,0:T(8,128)S(1)} %copy-done.8, bf16[8,256,128]{2,1,0:T(8,128)(2,1)S(1)} %copy-done.10, bf16[256,1024]{1,0:T(8,128)(2,1)S(1)} %copy-done.9, f32[1,128]{1,0:T(1,128)S(1)} %bitcast.15, bf16[1024,2048]{1,0:T(8,128)(2,1)S(1)} %copy-done), custom_call_target="tpu_custom_call" | custom-call | tf_op jit(solution)/shard_map/project/pallas_call | solution.py:299
  72.2 4.0 %all-to-all-start.3 = ((bf16[4,64,2048]{2,1,0:T(8,128)(2,1)}), bf16[4,64,2048]{2,1,0:T(8,128)(2,1)S(1)}, u32[]{:S(2)}, u32[]{:S(2)}) async-start(bf16[4,64,2048]{2,1,0:T(8,128)(2,1)} %project.1), calls=%async_computation.3 | async-start | bytes 2097152 | tf_op jit(solution)/shard_map/all_to_all | solution.py:523
  76.2 0.0 copy-done.15
  76.2 0.1 copy.22.experts_ref
  76.3 0.0 copy-done.16
  76.3 0.1 copy.23.weights_ref
  76.4 2.9 %route.1 = (bf16[6144,256]{1,0:T(8,128)(2,1)S(1)}, bf16[256,6144]{1,0:T(8,128)(2,1)S(1)}) custom-call(s32[64,10]{1,0:T(8,128)S(1)} %copy.22.experts_ref, f32[64,10]{1,0:T(8,128)S(1)} %copy.23.weights_ref), custom_call_target="tpu_custom_call" | custom-call | tf_op jit(solution)/shard_map/route/pallas_call | solution.py:346
  79.3 0.0 copy-start.4
  79.3 1.6 copy-done.4
  80.9 0.0 copy-start.6
  80.9 1.7 copy-done.6
  82.6 7.5 %all-to-all-done.3.parts_ref = bf16[4,64,2048]{2,1,0:T(8,128)(2,1)S(1)} async-done(((bf16[4,64,2048]{2,1,0:T(8,128)(2,1)}), bf16[4,64,2048]{2,1,0:T(8,128)(2,1)S(1)}, u32[]{:S(2)}, u32[]{:S(2)}) %all-to-all-start.3) | async-done | bytes 1048608 | tf_op jit(solution)/shard_map/all_to_all | solution.py:523
  90.1 0.0 copy-done.11
  90.1 0.0 copy-done.12
  90.1 0.0 copy-start.5
  90.1 1.9 copy-done.5
  92.0 2.1 dispatch.1
  94.0 0.0 copy-start.1
  94.1 0.0 copy-start.2
  94.1 0.0 copy-start.3
  94.1 81.3 %all_to_all.32 = bf16[128,48,512]{2,1,0:T(8,128)(2,1)S(1)} all-to-all(bf16[128,48,512]{2,1,0:T(8,128)(2,1)S(1)} %bitcast.13), channel_id=1, replica_groups=mesh['seq'=32,'exp'=4] {'seq','exp'}, dimensions={0} | all-to-all | bytes 12582912 | tf_op jit(solution)/shard_map/all_to_all | solution.py:469
  175.3 0.0 copy-done.1
  175.3 0.0 copy-done.2
  175.3 0.0 copy-done.3
  175.4 15.9 %experts_mlp.1 = bf16[6144,512]{1,0:T(8,128)(2,1)S(1)} custom-call(bf16[6144,512]{1,0:T(8,128)(2,1)S(1)} %bitcast.11, bf16[2,2048,512]{2,1,0:T(8,128)(2,1)S(1)} %copy-done.1, bf16[2,2048,512]{2,1,0:T(8,128)(2,1)S(1)} %copy-done.2, bf16[2,512,2048]{2,1,0:T(8,128)(2,1)S(1)} %copy-done.3), custom_call_target="tpu_custom_call" | custom-call | tf_op jit(solution)/shard_map/experts_mlp/pallas_call | solution.py:438
  191.3 0.0 copy-start.7
  191.3 79.3 %all_to_all.33 = bf16[128,48,512]{2,1,0:T(8,128)(2,1)S(1)} all-to-all(bf16[128,48,512]{2,1,0:T(8,128)(2,1)S(1)} %bitcast.12), channel_id=1, replica_groups=mesh['seq'=32,'exp'=4] {'seq','exp'}, dimensions={0} | all-to-all | bytes 12582912 | tf_op jit(solution)/shard_map/all_to_all | solution.py:469
  270.6 0.0 copy-done.7
  270.6 2.5 combine.1
  (1 shorter events, 0.0 us)
Async XLA Ops:
  0.6 66.5 %copy-start.13 = (f32[128]{0:T(128)S(1)}, f32[128]{0:T(128)}, u32[]{:S(2)}) copy-start(f32[128]{0:T(128)} %param.29) | copy-start | bytes 1540
  0.6 66.5 %copy-start.9 = (bf16[256,1024]{1,0:T(8,128)(2,1)S(1)}, bf16[256,1024]{1,0:T(8,128)(2,1)}, u32[]{:S(2)}) copy-start(bf16[256,1024]{1,0:T(8,128)(2,1)} %gate_ref.2) | copy-start | bytes 1572868
  2.8 6.2 %collective-permute-start = (bf16[8,2048]{1,0:T(8,128)(2,1)S(1)}, bf16[8,2048]{1,0:T(8,128)(2,1)S(1)}, u32[]{:S(2)}, u32[]{:S(2)}) collective-permute-start(bf16[8,2048]{1,0:T(8,128)(2,1)S(1)} %pad_maximum_fusion), channel_id=1, source_target_pairs={{0,4},{4,8},{8,12},{12,16},{16,20},{20,24},{24,28},{28,32},{32,36}... | collective-permute-start | bytes 98312 | tf_op jit(solution)/shard_map/ppermute | solution.py:497
  9.1 0.6 copy-start.14
  28.2 38.9 %copy-start.8 = (f32[8,256,128]{2,1,0:T(8,128)S(1)}, f32[8,256,128]{2,1,0:T(8,128)}, u32[]{:S(2)}) copy-start(f32[8,256,128]{2,1,0:T(8,128)} %get-tuple-element.16.local_ref) | copy-start | bytes 3145732
  28.2 38.9 %copy-start.10 = (bf16[8,256,128]{2,1,0:T(8,128)(2,1)S(1)}, bf16[8,256,128]{2,1,0:T(8,128)(2,1)}, u32[]{:S(2)}) copy-start(bf16[8,256,128]{2,1,0:T(8,128)(2,1)} %get-tuple-element.17.lift_ref) | copy-start | bytes 1572868
  45.3 9.9 %all-to-all-start.1 = ((bf16[4,256,128]{2,1,0:T(8,128)(2,1)}), bf16[4,256,128]{2,1,0:T(8,128)(2,1)S(1)}, u32[]{:S(2)}, u32[]{:S(2)}) async-start(bf16[4,256,128]{2,1,0:T(8,128)(2,1)} %get-tuple-element.13), calls=%async_computation.1 | async-start | bytes 524288 | tf_op jit(solution)/shard_map/all_to_all | solution.py:515
  67.1 2.2 copy-start
  69.3 6.8 %copy-start.15 = (s32[64,10]{0,1:T(8,128)S(1)}, s32[64,10]{0,1:T(8,128)}, u32[]{:S(2)}) copy-start(s32[64,10]{0,1:T(8,128)} %param.33) | copy-start | bytes 7684
  69.3 6.9 %copy-start.16 = (f32[64,10]{0,1:T(8,128)S(1)}, f32[64,10]{0,1:T(8,128)}, u32[]{:S(2)}) copy-start(f32[64,10]{0,1:T(8,128)} %param.34) | copy-start | bytes 7684
  69.3 20.7 %copy-start.11 = (bf16[64,2048]{1,0:T(8,128)(2,1)S(1)}, bf16[64,2048]{1,0:T(8,128)(2,1)}, u32[]{:S(2)}) copy-start(bf16[64,2048]{1,0:T(8,128)(2,1)} %res_ref.1) | copy-start | bytes 786436
  69.3 20.7 %copy-start.12 = (f32[2048]{0:T(1024)S(1)}, f32[2048]{0:T(1024)}, u32[]{:S(2)}) copy-start(f32[2048]{0:T(1024)} %param.32) | copy-start | bytes 24580
  72.2 17.9 %all-to-all-start.3 = ((bf16[4,64,2048]{2,1,0:T(8,128)(2,1)}), bf16[4,64,2048]{2,1,0:T(8,128)(2,1)S(1)}, u32[]{:S(2)}, u32[]{:S(2)}) async-start(bf16[4,64,2048]{2,1,0:T(8,128)(2,1)} %project.1), calls=%async_computation.3 | async-start | bytes 2097152 | tf_op jit(solution)/shard_map/all_to_all | solution.py:523
  79.3 1.6 copy-start.4
  80.9 1.7 copy-start.6
  90.1 1.9 copy-start.5
  94.0 81.3 %copy-start.1 = (bf16[2,2048,512]{2,1,0:T(8,128)(2,1)S(1)}, bf16[2,2048,512]{2,1,0:T(8,128)(2,1)}, u32[]{:S(2)}) copy-start(bf16[2,2048,512]{2,1,0:T(8,128)(2,1)} %gate_ref.3) | copy-start | bytes 12582916
  94.1 81.3 %copy-start.2 = (bf16[2,2048,512]{2,1,0:T(8,128)(2,1)S(1)}, bf16[2,2048,512]{2,1,0:T(8,128)(2,1)}, u32[]{:S(2)}) copy-start(bf16[2,2048,512]{2,1,0:T(8,128)(2,1)} %up_ref.1) | copy-start | bytes 12582916
  94.1 81.3 %copy-start.3 = (bf16[2,512,2048]{2,1,0:T(8,128)(2,1)S(1)}, bf16[2,512,2048]{2,1,0:T(8,128)(2,1)}, u32[]{:S(2)}) copy-start(bf16[2,512,2048]{2,1,0:T(8,128)(2,1)} %down_ref.1) | copy-start | bytes 12582916
  191.3 79.3 %copy-start.7 = (bf16[256,6144]{1,0:T(8,128)(2,1)S(1)}, bf16[256,6144]{1,0:T(8,128)(2,1)}, u32[]{:S(2)}) copy-start(bf16[256,6144]{1,0:T(8,128)(2,1)} %copy-done.6) | copy-start | bytes 9437188

commit v2 on v1

--- a/solution.py
+++ b/solution.py
@@ -10,6 +10,8 @@
 EPS = 1e-06
 HD = 128
 BLK = 128
+SUB = 16
+KH = 2
 TOK = 256
 HALO = 8
 SEQ = 32
@@ -48,9 +50,9 @@
 TN = ((0,), (0,))
 
 
-def conv_silu(ref, halo_ref, taps_ref, pad_ref):
+def conv_silu(ref, halo, taps_ref, pad_ref):
     width = ref.shape[1]
-    pad_ref[0:HALO, 0:width] = halo_ref[...].astype(f32)
+    pad_ref[0:HALO, 0:width] = halo.astype(f32)
     pad_ref[HALO : HALO + TOK, 0:width] = ref[...].astype(f32)
     run = taps_ref[0:1, :] * pad_ref[HALO - 3 : HALO - 3 + TOK, 0:width]
     for j in range(1, 4):
@@ -64,23 +66,37 @@
     )
 
 
-def inverses(couplings):
+def fill_spread(ref):
+    width = (SUB - 1) * BLK
+    src = iota((BLK, width), 0)
+    dst = iota((BLK, width), 1)
+    ref[...] = (src == SUB * ((dst % BLK) // SUB) + dst // BLK).astype(bf16)
+
+
+def inverses(couplings, spread_ref):
     count = len(couplings)
-    lane = iota((8, BLK), 1)
-    sub = iota((8, BLK), 0)
-    slabs = [[] for _ in range(count)]
-    for m in range(BLK // 8):
-        a = [c[8 * m : 8 * m + 8] for c in couplings]
-        t = [(lane == sub + 8 * m).astype(f32)] * count
-        for j in range(7):
-            t = [t[n] - a[n][:, 8 * m + j : 8 * m + j + 1] * t[n][j : j + 1, :] for n in range(count)]
-        for n in range(count):
-            slabs[n].append(t[n])
-    ts = [jnp.concatenate(x, axis=0) for x in slabs]
+    lane = iota((SUB, BLK), 1)
+    sub = iota((SUB, BLK), 0)
+    packs = []
+    for c in couplings:
+        pack = jnp.zeros((SUB, BLK), f32)
+        for m in range(BLK // SUB):
+            pack = jnp.where(lane // SUB == m, c[SUB * m : SUB * (m + 1)], pack)
+        packs.append(pack)
+    hi, lo = split(jnp.concatenate(packs, axis=0))
+    small = [(lane % SUB == sub).astype(f32)] * count
+    for j in range(SUB - 1):
+        span = slice(j * BLK, (j + 1) * BLK)
+        wide = dot(hi, spread_ref[:, span]) + dot(lo, spread_ref[:, span])
+        small = [t - wide[SUB * n : SUB * (n + 1)] * t[j : j + 1, :] for n, t in enumerate(small)]
+    ts = [
+        jnp.concatenate([jnp.where(lane // SUB == m, t, 0.0) for m in range(BLK // SUB)], axis=0)
+        for t in small
+    ]
     half = BLK // 2
     rows = iota((half, BLK), 0)
     cols = iota((half, BLK), 1)
-    size = 8
+    size = SUB
     while size < BLK:
         part = cols // size == 2 * (rows // size)
         zero = jnp.zeros((size, BLK), f32)
@@ -105,64 +121,80 @@
     return [split(t) for t in ts]
 
 
-def mixer_body(q_ref, k_ref, v_ref, hq_ref, hk_ref, hv_ref, bl_ref, dl_ref, rate_ref, cq_ref, ck_ref, cv_ref,
-               map_ref, local_ref, lift_ref, pad_ref, cum_ref, beta_ref):
+def mixer_body(q_ref, k_ref, v_ref, halo_ref, bl_ref, dl_ref, rate_ref, cq_ref, ck_ref, cv_ref,
+               map_ref, local_ref, lift_ref, pad_ref, cum_ref, beta_ref, spread_ref):
     step = pl.program_id(0)
     row = iota((BLK, BLK), 0)
     col = iota((BLK, BLK), 1)
-    x = dl_ref[...]
-    soft = jnp.maximum(x, 0.0) + jnp.log1p(jnp.exp(-jnp.abs(x)))
-    decay = jnp.maximum(-rate_ref[...] * soft, -110.0)
-    upper = (row <= col).astype(f32)
+
+    @pl.when(step == 0)
+    def _():
+        fill_spread(spread_ref)
+        x = dl_ref[...]
+        soft = jnp.maximum(x, 0.0) + jnp.log1p(jnp.exp(-jnp.abs(x)))
+        square = iota((8, 8), 0) == iota((8, 8), 1)
+        rate = jnp.sum(jnp.where(square, rate_ref[...], 0.0), axis=1, keepdims=True)
+        decay = jnp.maximum(-rate * soft, -110.0)
+        upper = (row <= col).astype(f32)
+        for b in range(2):
+            cum_ref[b] = lax.dot_general(decay[:, b * BLK : (b + 1) * BLK], upper, (((1,), (0,)), ((), ())),
+                                         precision=lax.Precision.HIGHEST, preferred_element_type=f32)
+            beta_ref[b] = 1.0 / (1.0 + jnp.exp(-bl_ref[:, b * BLK : (b + 1) * BLK]))
+
+    kw = KH * HD
+
+    def halo(at, width):
+        return halo_ref[:, pl.ds(pl.multiple_of(at + step * width, width), width)]
+
+    queries = conv_silu(q_ref, halo(0, kw), cq_ref, pad_ref)
+    keys = conv_silu(k_ref, halo(4 * HD, kw), ck_ref, pad_ref)
+    values = conv_silu(v_ref, halo(8 * HD, 2 * kw), cv_ref, pad_ref)
+    heads = 2 * KH
+    rows = {}
     for b in range(2):
-        cum_ref[b] = lax.dot_general(decay[:, b * BLK : (b + 1) * BLK], upper, (((1,), (0,)), ((), ())),
-                                     precision=lax.Precision.HIGHEST, preferred_element_type=f32)
-        beta_ref[b] = 1.0 / (1.0 + jnp.exp(-bl_ref[:, b * BLK : (b + 1) * BLK]))
-
-    queries = conv_silu(q_ref, hq_ref, cq_ref, pad_ref)
-    keys = conv_silu(k_ref, hk_ref, ck_ref, pad_ref)
-    keys = keys * lax.rsqrt(jnp.sum(keys * keys, axis=1, keepdims=True) + EPS)
-    values = conv_silu(v_ref, hv_ref, cv_ref, pad_ref)
-
-    rows = []
-    for b in range(2):
-        for i in range(2):
-            rows.append(cum_ref[b, pl.ds(2 * step + i, 1), :])
-            rows.append(beta_ref[b, pl.ds(2 * step + i, 1), :])
-    wide = jnp.concatenate(rows + [jnp.zeros((BLK - 8, BLK), f32)], axis=0)
-    tall = wide.T
+        for i in range(heads):
+            rows[b, i] = (
+                cum_ref[b, pl.ds(heads * step + i, 1), :],
+                beta_ref[b, pl.ds(heads * step + i, 1), :],
+            )
+    keyed = [(b, i) for b in range(2) for i in range(heads)]
+    wide = [r for key in keyed for r in rows[key]]
+    tall = jnp.concatenate(wide + [jnp.zeros((BLK - len(wide), BLK), f32)], axis=0).T
 
     res = {}
-    keyed = [(b, i) for b in range(2) for i in range(2)]
-    grams, scores, masks, couplings = {}, {}, {}, []
-    for b in range(2):
-        kb = split(keys[b * BLK : (b + 1) * BLK])
-        grams[b] = dot3(kb, kb, NT)
-        scores[b] = dot(queries[b * BLK : (b + 1) * BLK].astype(bf16), kb[0], NT)
-    for b, i in keyed:
-        at = 2 * (2 * b + i)
-        spread = tall[:, at : at + 1] - rows[at]
+    qs, ks, grams, scores, masks, couplings = {}, {}, {}, {}, {}, []
+    for c in range(KH):
+        unit = keys[:, c * HD : (c + 1) * HD]
+        unit = unit * lax.rsqrt(jnp.sum(unit * unit, axis=1, keepdims=True) + EPS)
+        for b in range(2):
+            qs[b, c] = queries[b * BLK : (b + 1) * BLK, c * HD : (c + 1) * HD]
+            ks[b, c] = unit[b * BLK : (b + 1) * BLK]
+            kb = split(ks[b, c])
+            grams[b, c] = dot3(kb, kb, NT)
+            scores[b, c] = dot(qs[b, c].astype(bf16), kb[0], NT)
+    for n, (b, i) in enumerate(keyed):
+        spread = tall[:, 2 * n : 2 * n + 1] - rows[b, i][0]
         masks[b, i] = jnp.where(row >= col, jnp.exp(jnp.where(row >= col, spread, 0.0)), 0.0)
-        couplings.append(jnp.where(row > col, tall[:, at + 1 : at + 2] * grams[b] * masks[b, i], 0.0))
-    invs = dict(zip(keyed, inverses(couplings)))
-    for b, i in keyed:
-        at = 2 * (2 * b + i)
-        cum_c = tall[:, at : at + 1]
-        beta_c = tall[:, at + 1 : at + 2]
-        qb = queries[b * BLK : (b + 1) * BLK]
-        kb = keys[b * BLK : (b + 1) * BLK]
+        couplings.append(
+            jnp.where(row > col, tall[:, 2 * n + 1 : 2 * n + 2] * grams[b, i // 2] * masks[b, i], 0.0)
+        )
+    invs = inverses(couplings, spread_ref)
+    for n, (b, i) in enumerate(keyed):
+        cum_c = tall[:, 2 * n : 2 * n + 1]
+        beta_c = tall[:, 2 * n + 1 : 2 * n + 2]
+        qb, kb = qs[b, i // 2], ks[b, i // 2]
         vb = values[b * BLK : (b + 1) * BLK, i * HD : (i + 1) * HD]
         grow = jnp.exp(cum_c)
         last = cum_c[BLK - 1 : BLK, :]
         key_tail = (kb * jnp.exp(last - cum_c)).astype(bf16)
         rhs = jnp.concatenate([beta_c * vb, (beta_c * grow) * kb], axis=1)
-        solved = dot3(invs[b, i], split(rhs)).astype(bf16)
-        near = dot((scores[b] * masks[b, i]).astype(bf16), solved)
+        solved = dot3(invs[n], split(rhs)).astype(bf16)
+        near = dot((scores[b, i // 2] * masks[b, i]).astype(bf16), solved)
         local = near[:, :HD]
         lift = grow * qb - near[:, HD:]
         both = dot(solved, key_tail, TN)
         res[b, i] = (local, lift, jnp.exp(last), both)
-    for i in range(2):
+    for i in range(heads):
         l0, f0, t0, both0 = res[0, i]
         l1, f1, t1, both1 = res[1, i]
         w0, gone0 = both0[:HD], both0[HD:]
@@ -181,28 +213,27 @@
 
 
 def mixer_blocks(q, k, v, halo, beta_t, decay_t, rate, cq, ck, cv):
-    w = HD
+    w = KH * HD
+    heads = 2 * KH
+    cols = lambda s: (0, s)
     return pl.pallas_call(
         mixer_body,
-        grid=(4,),
+        grid=(4 // KH,),
         in_specs=[
-            pl.BlockSpec((TOK, w), lambda s: (0, s)),
-            pl.BlockSpec((TOK, w), lambda s: (0, s)),
-            pl.BlockSpec((TOK, 2 * w), lambda s: (0, s)),
-            pl.BlockSpec((HALO, w), lambda s: (0, s)),
-            pl.BlockSpec((HALO, w), lambda s: (0, 4 + s)),
-            pl.BlockSpec((HALO, 2 * w), lambda s: (0, 4 + s)),
-            pl.BlockSpec((8, TOK), lambda s: (0, 0)),
-            pl.BlockSpec((8, TOK), lambda s: (0, 0)),
-            pl.BlockSpec((8, 1), lambda s: (0, 0)),
-            pl.BlockSpec((4, w), lambda s: (0, s)),
-            pl.BlockSpec((4, w), lambda s: (0, s)),
-            pl.BlockSpec((4, 2 * w), lambda s: (0, s)),
+            pl.BlockSpec((TOK, w), cols),
+            pl.BlockSpec((TOK, w), cols),
+            pl.BlockSpec((TOK, 2 * w), cols),
+        ]
+        + in_vmem(4)
+        + [
+            pl.BlockSpec((4, w), cols),
+            pl.BlockSpec((4, w), cols),
+            pl.BlockSpec((4, 2 * w), cols),
         ],
         out_specs=[
-            pl.BlockSpec((2, 2 * HD, HD), lambda s: (s, 0, 0)),
-            pl.BlockSpec((2, TOK, HD), lambda s: (s, 0, 0)),
-            pl.BlockSpec((2, TOK, HD), lambda s: (s, 0, 0)),
+            pl.BlockSpec((heads, 2 * HD, HD), lambda s: (s, 0, 0)),
+            pl.BlockSpec((heads, TOK, HD), lambda s: (s, 0, 0)),
+            pl.BlockSpec((heads, TOK, HD), lambda s: (s, 0, 0)),
         ],
         out_shape=[
             jax.ShapeDtypeStruct((NEAR, 2 * HD, HD), bf16),
@@ -210,13 +241,32 @@
             jax.ShapeDtypeStruct((8, TOK, HD), bf16),
         ],
         scratch_shapes=[
-            pltpu.VMEM((TOK + HALO, 2 * HD), f32),
+            pltpu.VMEM((TOK + HALO, 2 * w), f32),
             pltpu.VMEM((2, 8, BLK), f32),
             pltpu.VMEM((2, 8, BLK), f32),
-        ],
-        compiler_params=pltpu.CompilerParams(vmem_limit_bytes=VMEM),
+            pltpu.VMEM((BLK, (SUB - 1) * BLK), bf16),
+        ],
+        compiler_params=vmem(56),
         name="mixer_blocks",
-    )(q, k, v, halo, halo, halo, beta_t, decay_t, rate, cq, ck, cv)
+    )(q, k, v, halo, beta_t, decay_t, rate, cq, ck, cv)
+
+
+def edge_body(q_ref, k_ref, v_ref, out_ref):
+    out_ref[:, 0 : 4 * HD] = q_ref[...]
+    out_ref[:, 4 * HD : 8 * HD] = k_ref[...]
+    out_ref[:, 8 * HD : 16 * HD] = v_ref[...]
+
+
+def edge_rows(q, k, v):
+    last = lambda n: (TOK // HALO - 1, 0)
+    return pl.pallas_call(
+        edge_body,
+        grid=(1,),
+        in_specs=[pl.BlockSpec((HALO, a.shape[1]), last) for a in (q, k, v)],
+        out_specs=pl.BlockSpec((HALO, 2048), lambda n: (0, 0)),
+        out_shape=jax.ShapeDtypeStruct((HALO, 2048), bf16),
+        name="edge_rows",
+    )(q, k, v)
 
 
 def in_vmem(count):
@@ -236,8 +286,7 @@
         here = in_ref[j]
         both = dot(hi, here[:HD]) + dot(lo, here[:HD])
         both = jnp.concatenate([both[:HD], both[HD:] + here[HD:].astype(f32)], axis=0)
-    for g in range(FAR):
-        all_ref[g] = both.astype(bf16)
+    all_ref[...] = both.astype(bf16)
 
 
 def near_scan(maps):
@@ -247,39 +296,33 @@
         out_shape=[
             jax.ShapeDtypeStruct((NEAR - 1, HD, HD), bf16),
             jax.ShapeDtypeStruct((NEAR - 1, HD, HD), f32),
-            jax.ShapeDtypeStruct((FAR, 2 * HD, HD), bf16),
+            jax.ShapeDtypeStruct((2 * HD, HD), bf16),
         ],
         compiler_params=vmem(8),
         name="near_scan",
     )(maps)
 
 
-def far_body(at_ref, all_ref, map_ref, mem_ref, out_ref):
-    state = jnp.zeros((HD, HD), f32)
-    entry = state
-    for g in range(FAR - 1):
-        if g == 0:
-            state = all_ref[0, HD:].astype(f32)
-        else:
-            hi, lo = split(state)
-            here = all_ref[g]
-            state = dot(hi, here[:HD]) + dot(lo, here[:HD]) + here[HD:].astype(f32)
-        entry = jnp.where(at_ref[0] == g + 1, state, entry)
-    hi, lo = split(entry)
+def far_body(near_ref, next_ref, last_ref, w_ref, map_ref, mem_ref, out_ref):
+    state = last_ref[HD:].astype(f32)
+    for ref in (next_ref, near_ref):
+        hi, lo = split(state)
+        state = dot(hi, ref[:HD]) + dot(lo, ref[:HD]) + ref[HD:].astype(f32)
+    hi, lo = split(state)
     out_ref[0] = hi
     for j in range(1, NEAR):
         m = map_ref[j - 1]
         out_ref[j] = (dot(hi, m) + dot(lo, m) + mem_ref[j - 1]).astype(bf16)
 
 
-def far_scan(place, totals, maps, memories):
+def far_scan(totals, weight, maps, memories):
     return pl.pallas_call(
         far_body,
-        in_specs=[pl.BlockSpec(memory_space=pltpu.SMEM)] + in_vmem(3),
+        in_specs=in_vmem(3) + [pl.BlockSpec(memory_space=pl.ANY)] + in_vmem(2),
         out_shape=jax.ShapeDtypeStruct((NEAR, HD, HD), bf16),
-        compiler_params=vmem(8),
+        compiler_params=vmem(50),
         name="far_scan",
-    )(place, totals, maps, memories)
+    )(*totals, weight, maps, memories)
 
 
 def project_body(s_ref, local_ref, lift_ref, gate_ref, gain_ref, w_ref, out_ref, norm_ref):
@@ -306,7 +349,7 @@
     )(states, local, lift, gate, gain, weight)
 
 
-def route_body(experts_ref, weights_ref, pick_ref, part_ref, slot_ref, share_ref):
+def route_body(experts_ref, weights_ref, slot_ref, part_ref, share_ref):
     ids = experts_ref[...]
     weights = weights_ref[...]
     shares = weights / jnp.sum(weights, axis=1, keepdims=True)
@@ -334,11 +377,10 @@
     shs = share_ref[...]
     lane2 = iota((CH, NQ * ROWS), 1).astype(f32)
     for g in range(DEV // 8):
-        tall = []
-        for d in range(8 * g, 8 * g + 8):
-            hit = slots[:, d : d + 1] == lane2
-            pick_ref[d * CH : (d + 1) * CH, :] = jnp.where(hit, 1.0, 0.0).astype(bf16)
-            tall.append(jnp.where(hit, shs[:, d : d + 1], 0.0))
+        tall = [
+            jnp.where(slots[:, d : d + 1] == lane2, shs[:, d : d + 1], 0.0)
+            for d in range(8 * g, 8 * g + 8)
+        ]
         part_ref[:, g * 8 * CH : (g + 1) * 8 * CH] = jnp.concatenate(tall, axis=0).T.astype(bf16)
 
 
@@ -346,16 +388,16 @@
     return pl.pallas_call(
         route_body,
         out_shape=[
-            jax.ShapeDtypeStruct((DEV * CH, NQ * ROWS), bf16),
+            jax.ShapeDtypeStruct((CH, DEV), f32),
             jax.ShapeDtypeStruct((NQ * ROWS, DEV * CH), bf16),
         ],
-        scratch_shapes=[pltpu.VMEM((CH, DEV), f32), pltpu.VMEM((CH, DEV), f32)],
+        scratch_shapes=[pltpu.VMEM((CH, DEV), f32)],
         compiler_params=vmem(16),
         name="route",
     )(experts, weights)
 
 
-def dispatch_body(parts_ref, res_ref, gain_ref, pick_ref, mix_ref, out_ref, stack_ref):
+def dispatch_body(parts_ref, res_ref, gain_ref, slot_ref, mix_ref, out_ref, stack_ref):
     total = parts_ref[0].astype(f32)
     for e in range(1, EXP):
         total = total + parts_ref[e].astype(f32)
@@ -366,14 +408,21 @@
     normed = (m * lax.rsqrt(ms + EPS) * gain_ref[...]).astype(bf16)
     for q in range(NQ):
         stack_ref[q * ROWS : (q + 1) * ROWS, :] = normed[:, q * QW : (q + 1) * QW]
-    step = DEV * CH // 8
-    for n in range(8):
-        out_ref[n * step : (n + 1) * step, :] = dot(
-            pick_ref[n * step : (n + 1) * step, :], stack_ref[...]
-        ).astype(bf16)
-
-
-def dispatch(parts, residual, gain, pick):
+    slots = slot_ref[...]
+    lane = iota((CH, NQ * ROWS), 1).astype(f32)
+    each = 16
+    for n in range(DEV // each):
+        pick = jnp.concatenate(
+            [
+                jnp.where(slots[:, d : d + 1] == lane, 1.0, 0.0).astype(bf16)
+                for d in range(n * each, (n + 1) * each)
+            ],
+            axis=0,
+        )
+        out_ref[n * each * CH : (n + 1) * each * CH, :] = dot(pick, stack_ref[...]).astype(bf16)
+
+
+def dispatch(parts, residual, gain, slots):
     return pl.pallas_call(
         dispatch_body,
         in_specs=in_vmem(4),
@@ -384,7 +433,7 @@
         scratch_shapes=[pltpu.VMEM((NQ * ROWS, QW), bf16)],
         compiler_params=vmem(16),
         name="dispatch",
-    )(parts, residual, gain, pick)
+    )(parts, residual, gain, slots)
 
 
 GS = 4
@@ -411,7 +460,7 @@
                 x_ref[e, pl.ds(2 * PR * i, 2 * PR), q * QW : (q + 1) * QW] = both
         return 0
 
-    lax.fori_loop(0, pairs, load, 0, unroll=2)
+    lax.fori_loop(0, pairs, load, 0, unroll=4)
     for e in range(2):
         x = x_ref[e]
         g = dot(x, gate_ref[e])
@@ -431,7 +480,7 @@
             out_ref[pl.ds(2 * GR * i + GR * h, GR), :] = dot(perm_t, z).astype(bf16)
         return 0
 
-    lax.fori_loop(0, pairs, store, 0, unroll=2)
+    lax.fori_loop(0, pairs, store, 0, unroll=4)
 
 
 def experts_mlp(arrived, gate, up, down):
@@ -491,11 +540,9 @@
     expert_up,
     expert_down,
 ):
-    edge = jnp.concatenate(
-        [a[TOK - HALO :] for a in (query_proj, key_proj, value_proj)], axis=1
-    )
+    edge = edge_rows(query_proj, key_proj, value_proj)
     halo = lax.ppermute(edge, "seq", [(s, s + 1) for s in range(SEQ - 1)])
-    pick, share = route(route_experts, route_weights)
+    slots, share = route(route_experts, route_weights)
     maps, local, lift = mixer_blocks(
         query_proj,
         key_proj,
@@ -503,25 +550,26 @@
         halo,
         beta_logit.T,
         decay_logit.T,
-        decay_rate[:, None],
+        decay_rate[None, :],
         conv_query,
         conv_key,
         conv_value,
     )
     near = [[g * NEAR + j for j in range(NEAR)] for g in range(FAR)]
-    far = [[g * NEAR + j for g in range(FAR)] for j in range(NEAR)]
-
-    def swap(array, groups):
-        return lax.all_to_all(array, "seq", split_axis=0, concat_axis=0, axis_index_groups=groups, tiled=True)
-
-    before, memories, totals = near_scan(swap(maps, near))
-    place = (lax.axis_index("seq") // NEAR).astype(jnp.int32).reshape(1)
-    states = swap(far_scan(place, swap(totals, far), before, memories), near)
+
+    def swap(array):
+        return lax.all_to_all(array, "seq", split_axis=0, concat_axis=0, axis_index_groups=near, tiled=True)
+
+    before, memories, total = near_scan(swap(maps))
+    totals = [
+        lax.ppermute(total, "seq", [(s, s + k * NEAR) for s in range(SEQ - k * NEAR)]) for k in range(1, FAR)
+    ]
+    states = swap(far_scan(totals, output_weight, before, memories))
     parts = project(
         states, local, lift, result_valve_maps, norm_gain[None, :], output_weight
     )
     parts = lax.all_to_all(parts, "exp", split_axis=0, concat_axis=0, tiled=True)
-    mixer_out, outgoing = dispatch(parts, residual, post_gain[None, :], pick)
+    mixer_out, outgoing = dispatch(parts, residual, post_gain[None, :], slots)
     finished = experts_mlp(exchange(outgoing), expert_gate, expert_up, expert_down)
     return (mixer_out, combine(share, exchange(finished)))
 

time: 274 us -> 263 us (0.960)
  local copies, waits for them, and re-layouts: 11.7 us -> 2.5 us
  Pallas kernels: 47.2 us -> 41.8 us
  starting transfers between devices: 13.3 us -> 17.5 us
    ppermute x0 -> x3, starting transfers between devices: none -> 8.61 us  [body(): lax.ppermute(total, 'seq', [(s, s + k * NEAR) for s in range(SEQ - k * NE...]
    unnamed x36 -> x32, local copies, waits for them, and re-layouts: 8.22 us -> 2.5 us
    all_to_all x1 -> x0, waiting for transfers between devices: 5.53 us -> none  [swap(): lax.all_to_all(array, 'seq', split_axis=0, concat_axis=0, axis_index_grou...]
    all_to_all x1 -> x0, starting transfers between devices: 4.38 us -> none  [swap(): lax.all_to_all(array, 'seq', split_axis=0, concat_axis=0, axis_index_grou...]
    pallas_call x3 -> x4, Pallas kernels: 22 us -> 18.7 us  [the longest x1 13.8 us: mixer_blocks(): pl.pallas_call(mixer_body, grid=(4 // KH,), in_specs=[pl.BlockSpec((TOK,...]
  transfers between devices with their start and end apart: 3 -> 5, of which waited for: 2 -> 3; matrix products, arithmetic and copies ran while one was open for 1% -> 0% of each run, Pallas kernels for 1% -> 1%
where the time goes in v2:
time: 263 us
  blocking collectives  188 us (71%)
  Pallas kernels  41.8 us (16%)
  starting transfers between devices  17.5 us (7%)
  waiting for transfers between devices  11.7 us (4%)
    all_to_all x2, blocking collectives, exchange(): lax.all_to_all(chunks, ('seq', 'exp'), split_axis=0, concat_axis=0, tiled...  162 us
    all_to_all x2, blocking collectives, swap(): lax.all_to_all(array, 'seq', split_axis=0, concat_axis=0, axis_index_grou...  26.5 us
    pallas_call x1, Pallas kernels, experts_mlp(): pl.pallas_call(expert_body, in_specs=in_vmem(4), out_shape=jax.ShapeDtype...  14.7 us
    pallas_call x1, Pallas kernels, mixer_blocks(): pl.pallas_call(mixer_body, grid=(4 // KH,), in_specs=[pl.BlockSpec((TOK,...  13.8 us
    all_to_all x1, waiting for transfers between devices, body(): lax.all_to_all(parts, 'exp', split_axis=0, concat_axis=0, tiled=True)  9.1 us
    ppermute x3, starting transfers between devices, body(): lax.ppermute(total, 'seq', [(s, s + k * NEAR) for s in range(SEQ - k * NE...  8.61 us
  transfers between devices with their start and end apart: 5, of which 3 were waited for; matrix products, arithmetic and copies ran while one was open for 0% of the time, Pallas kernels for 1%

profile of v2, /device:TPU:1, one launch (start us, length us, event | category | flops | bytes accessed | tf_op | source)
XLA Modules:
  0.0 262.6 jit_solution(14074423810755346761)
XLA Ops:
  0.6 1.4 edge_rows.1
  2.0 4.9 %collective-permute-start = (bf16[8,2048]{1,0:T(8,128)(2,1)}, bf16[8,2048]{1,0:T(8,128)(2,1)S(1)}, u32[]{:S(2)}, u32[]{:S(2)}) collective-permute-start(bf16[8,2048]{1,0:T(8,128)(2,1)} %edge_rows.1), channel_id=1, source_target_pairs={{0,4},{4,8},{8,12},{12,16},{16,20},{20,24},{24,28},{28,32},{32,36}... | collective-permute-start | bytes 98312 | tf_op jit(solution)/shard_map/ppermute | solution.py:544
  6.9 1.3 collective-permute-done.halo_ref
  8.2 0.0 copy-start.12
  8.2 0.6 copy-done.12
  8.9 0.0 copy-start
  8.9 0.0 copy-start.7
  8.9 0.0 copy-start.11
  8.9 13.8 %mixer_blocks.1 = (bf16[8,256,128]{2,1,0:T(8,128)(2,1)}, f32[8,256,128]{2,1,0:T(8,128)}, bf16[8,256,128]{2,1,0:T(8,128)(2,1)}) custom-call(bf16[256,512]{1,0:T(8,128)(2,1)} %q_ref.3, bf16[256,512]{1,0:T(8,128)(2,1)} %k_ref.3, bf16[256,1024]{1,0:T(8,128)(2,1)} %v_ref.3, bf16[8,2048]{1,0:T(8,128)(2,1)} %copy-done.12, f32[8,256]{1,0:T(8,128)} %bitcast.15, ...), custom_call_target="tpu_custom_call" | custom-call | tf_op jit(solution)/shard_map/mixer_blocks/pallas_call | solution.py:219
  22.7 0.0 copy-start.6
  22.7 0.0 copy-start.8
  22.7 15.5 %all_to_all.25.in_ref = bf16[8,256,128]{2,1,0:T(8,128)(2,1)S(1)} all-to-all(bf16[8,256,128]{2,1,0:T(8,128)(2,1)} %get-tuple-element.12), channel_id=1, replica_groups={{0,4,8,12,16,20,24,28},{32,36,40,44,48,52,56,60},{64,68,72,76,80,84,88,..., dimensions={0} | all-to-all | bytes 1048576 | tf_op jit(solution)/shard_map/all_to_all | solution.py:561
  38.2 1.1 near_scan.1
  39.3 4.8 %collective-permute-start.3 = (bf16[256,128]{1,0:T(8,128)(2,1)S(1)}, bf16[256,128]{1,0:T(8,128)(2,1)S(1)}, u32[]{:S(2)}, u32[]{:S(2)}) collective-permute-start(bf16[256,128]{1,0:T(8,128)(2,1)S(1)} %get-tuple-element.13), channel_id=1, source_target_pairs={{0,96},{4,100},{8,104},{12,108},{16,112},{20,116},{24,120},{28,124... | collective-permute-start | bytes 196616 | tf_op jit(solution)/shard_map/ppermute | solution.py:565
  44.1 1.3 collective-permute-start.2
  45.4 2.5 collective-permute-start.1
  47.9 0.0 collective-permute-done.3.last_ref
  47.9 0.0 collective-permute-done.2.next_ref
  48.0 1.3 collective-permute-done.1.near_ref
  49.2 0.6 far_scan.1
  49.8 11.1 %all_to_all.26.s_ref = bf16[8,128,128]{2,1,0:T(8,128)(2,1)S(1)} all-to-all(bf16[8,128,128]{2,1,0:T(8,128)(2,1)S(1)} %far_scan.1), channel_id=1, replica_groups={{0,4,8,12,16,20,24,28},{32,36,40,44,48,52,56,60},{64,68,72,76,80,84,88,..., dimensions={0} | all-to-all | bytes 524288 | tf_op jit(solution)/shard_map/all_to_all | solution.py:561
  60.9 0.0 copy-done
  60.9 0.0 copy-done.7
  60.9 0.0 copy-done.11
  60.9 0.0 copy-done.6
  60.9 0.0 copy-done.8
  60.9 0.0 copy-start.13
  60.9 0.0 copy-start.14
  60.9 0.0 copy-start.9
  60.9 0.0 copy-start.10
  60.9 2.8 %project.1 = bf16[4,64,2048]{2,1,0:T(8,128)(2,1)} custom-call(bf16[8,128,128]{2,1,0:T(8,128)(2,1)S(1)} %all_to_all.26.s_ref, f32[8,256,128]{2,1,0:T(8,128)S(1)} %copy-done.6, bf16[8,256,128]{2,1,0:T(8,128)(2,1)S(1)} %copy-done.8, bf16[256,1024]{1,0:T(8,128)(2,1)S(1)} %copy-done.7, f32[1,128]{1,0:T(1,128)S(1)} %bitcast.14, bf16[1024,2048]{1,0:T(8,128)(2,1)S(1)} %copy-done), custom_call_target="tpu_custom_call" | custom-call | tf_op jit(solution)/shard_map/project/pallas_call | solution.py:342
  63.7 4.0 %all-to-all-start.2 = ((bf16[4,64,2048]{2,1,0:T(8,128)(2,1)}), bf16[4,64,2048]{2,1,0:T(8,128)(2,1)S(1)}, u32[]{:S(2)}, u32[]{:S(2)}) async-start(bf16[4,64,2048]{2,1,0:T(8,128)(2,1)} %project.1), calls=%async_computation.2 | async-start | bytes 2097152 | tf_op jit(solution)/shard_map/all_to_all | solution.py:571
  67.7 0.0 copy-done.13
  67.7 0.1 copy.21.experts_ref
  67.8 0.0 copy-done.14
  67.8 0.1 copy.22.weights_ref
  67.9 2.9 %route.1 = (f32[48,128]{1,0:T(8,128)S(1)}, bf16[256,6144]{1,0:T(8,128)(2,1)S(1)}) custom-call(s32[64,10]{1,0:T(8,128)S(1)} %copy.21.experts_ref, f32[64,10]{1,0:T(8,128)S(1)} %copy.22.weights_ref), custom_call_target="tpu_custom_call" | custom-call | tf_op jit(solution)/shard_map/route/pallas_call | solution.py:388
  70.8 0.0 copy-start.4
  70.8 1.6 copy-done.4
  72.5 9.1 %all-to-all-done.2.parts_ref = bf16[4,64,2048]{2,1,0:T(8,128)(2,1)S(1)} async-done(((bf16[4,64,2048]{2,1,0:T(8,128)(2,1)}), bf16[4,64,2048]{2,1,0:T(8,128)(2,1)S(1)}, u32[]{:S(2)}, u32[]{:S(2)}) %all-to-all-start.2) | async-done | bytes 1048608 | tf_op jit(solution)/shard_map/all_to_all | solution.py:571
  81.6 0.0 copy-done.9
  81.6 0.0 copy-done.10
  81.6 2.1 dispatch.1
  83.7 0.0 copy-start.1
  83.7 0.0 copy-start.2
  83.7 0.0 copy-start.3
  83.7 82.4 %all_to_all.27 = bf16[128,48,512]{2,1,0:T(8,128)(2,1)S(1)} all-to-all(bf16[128,48,512]{2,1,0:T(8,128)(2,1)S(1)} %bitcast.12), channel_id=1, replica_groups=mesh['seq'=32,'exp'=4] {'seq','exp'}, dimensions={0} | all-to-all | bytes 12582912 | tf_op jit(solution)/shard_map/all_to_all | solution.py:518
  166.1 0.0 copy-done.1
  166.1 0.0 copy-done.2
  166.1 0.0 copy-done.3
  166.1 14.7 %experts_mlp.1 = bf16[6144,512]{1,0:T(8,128)(2,1)S(1)} custom-call(bf16[6144,512]{1,0:T(8,128)(2,1)S(1)} %bitcast.10, bf16[2,2048,512]{2,1,0:T(8,128)(2,1)S(1)} %copy-done.1, bf16[2,2048,512]{2,1,0:T(8,128)(2,1)S(1)} %copy-done.2, bf16[2,512,2048]{2,1,0:T(8,128)(2,1)S(1)} %copy-done.3), custom_call_target="tpu_custom_call" | custom-call | tf_op jit(solution)/shard_map/experts_mlp/pallas_call | solution.py:487
  180.8 0.0 copy-start.5
  180.8 79.3 %all_to_all.28 = bf16[128,48,512]{2,1,0:T(8,128)(2,1)S(1)} all-to-all(bf16[128,48,512]{2,1,0:T(8,128)(2,1)S(1)} %bitcast.11), channel_id=1, replica_groups=mesh['seq'=32,'exp'=4] {'seq','exp'}, dimensions={0} | all-to-all | bytes 12582912 | tf_op jit(solution)/shard_map/all_to_all | solution.py:518
  260.1 0.0 copy-done.5
  260.1 2.5 combine.1
Async XLA Ops:
  2.0 6.2 %collective-permute-start = (bf16[8,2048]{1,0:T(8,128)(2,1)}, bf16[8,2048]{1,0:T(8,128)(2,1)S(1)}, u32[]{:S(2)}, u32[]{:S(2)}) collective-permute-start(bf16[8,2048]{1,0:T(8,128)(2,1)} %edge_rows.1), channel_id=1, source_target_pairs={{0,4},{4,8},{8,12},{12,16},{16,20},{20,24},{24,28},{28,32},{32,36}... | collective-permute-start | bytes 98312 | tf_op jit(solution)/shard_map/ppermute | solution.py:544
  8.2 0.6 copy-start.12
  8.9 52.0 %copy-start = (bf16[1024,2048]{1,0:T(8,128)(2,1)S(1)}, bf16[1024,2048]{1,0:T(8,128)(2,1)}, u32[]{:S(2)}) copy-start(bf16[1024,2048]{1,0:T(8,128)(2,1)} %w_ref.3) | copy-start | bytes 12582916
  8.9 52.0 %copy-start.7 = (bf16[256,1024]{1,0:T(8,128)(2,1)S(1)}, bf16[256,1024]{1,0:T(8,128)(2,1)}, u32[]{:S(2)}) copy-start(bf16[256,1024]{1,0:T(8,128)(2,1)} %gate_ref.2) | copy-start | bytes 1572868
  8.9 52.0 %copy-start.11 = (f32[128]{0:T(128)S(1)}, f32[128]{0:T(128)}, u32[]{:S(2)}) copy-start(f32[128]{0:T(128)} %param.29) | copy-start | bytes 1540
  22.7 38.2 %copy-start.6 = (f32[8,256,128]{2,1,0:T(8,128)S(1)}, f32[8,256,128]{2,1,0:T(8,128)}, u32[]{:S(2)}) copy-start(f32[8,256,128]{2,1,0:T(8,128)} %get-tuple-element.16.local_ref) | copy-start | bytes 3145732
  22.7 38.2 %copy-start.8 = (bf16[8,256,128]{2,1,0:T(8,128)(2,1)S(1)}, bf16[8,256,128]{2,1,0:T(8,128)(2,1)}, u32[]{:S(2)}) copy-start(bf16[8,256,128]{2,1,0:T(8,128)(2,1)} %get-tuple-element.17.lift_ref) | copy-start | bytes 1572868
  39.3 8.6 %collective-permute-start.3 = (bf16[256,128]{1,0:T(8,128)(2,1)S(1)}, bf16[256,128]{1,0:T(8,128)(2,1)S(1)}, u32[]{:S(2)}, u32[]{:S(2)}) collective-permute-start(bf16[256,128]{1,0:T(8,128)(2,1)S(1)} %get-tuple-element.13), channel_id=1, source_target_pairs={{0,96},{4,100},{8,104},{12,108},{16,112},{20,116},{24,120},{28,124... | collective-permute-start | bytes 196616 | tf_op jit(solution)/shard_map/ppermute | solution.py:565
  44.1 3.8 %collective-permute-start.2 = (bf16[256,128]{1,0:T(8,128)(2,1)S(1)}, bf16[256,128]{1,0:T(8,128)(2,1)S(1)}, u32[]{:S(2)}, u32[]{:S(2)}) collective-permute-start(bf16[256,128]{1,0:T(8,128)(2,1)S(1)} %get-tuple-element.13), channel_id=1, source_target_pairs={{0,64},{4,68},{8,72},{12,76},{16,80},{20,84},{24,88},{28,92},{32,9... | collective-permute-start | bytes 196616 | tf_op jit(solution)/shard_map/ppermute | solution.py:565
  45.4 3.8 %collective-permute-start.1 = (bf16[256,128]{1,0:T(8,128)(2,1)S(1)}, bf16[256,128]{1,0:T(8,128)(2,1)S(1)}, u32[]{:S(2)}, u32[]{:S(2)}) collective-permute-start(bf16[256,128]{1,0:T(8,128)(2,1)S(1)} %get-tuple-element.13), channel_id=1, source_target_pairs={{0,32},{4,36},{8,40},{12,44},{16,48},{20,52},{24,56},{28,60},{32,6... | collective-permute-start | bytes 196616 | tf_op jit(solution)/shard_map/ppermute | solution.py:565
  60.9 6.8 %copy-start.13 = (s32[64,10]{0,1:T(8,128)S(1)}, s32[64,10]{0,1:T(8,128)}, u32[]{:S(2)}) copy-start(s32[64,10]{0,1:T(8,128)} %param.33) | copy-start | bytes 7684
  60.9 6.9 %copy-start.14 = (f32[64,10]{0,1:T(8,128)S(1)}, f32[64,10]{0,1:T(8,128)}, u32[]{:S(2)}) copy-start(f32[64,10]{0,1:T(8,128)} %param.34) | copy-start | bytes 7684
  60.9 20.7 %copy-start.9 = (bf16[64,2048]{1,0:T(8,128)(2,1)S(1)}, bf16[64,2048]{1,0:T(8,128)(2,1)}, u32[]{:S(2)}) copy-start(bf16[64,2048]{1,0:T(8,128)(2,1)} %res_ref.1) | copy-start | bytes 786436
  60.9 20.6 %copy-start.10 = (f32[2048]{0:T(1024)S(1)}, f32[2048]{0:T(1024)}, u32[]{:S(2)}) copy-start(f32[2048]{0:T(1024)} %param.32) | copy-start | bytes 24580
  63.7 17.9 %all-to-all-start.2 = ((bf16[4,64,2048]{2,1,0:T(8,128)(2,1)}), bf16[4,64,2048]{2,1,0:T(8,128)(2,1)S(1)}, u32[]{:S(2)}, u32[]{:S(2)}) async-start(bf16[4,64,2048]{2,1,0:T(8,128)(2,1)} %project.1), calls=%async_computation.2 | async-start | bytes 2097152 | tf_op jit(solution)/shard_map/all_to_all | solution.py:571
  70.8 1.6 copy-start.4
  83.7 82.4 %copy-start.1 = (bf16[2,2048,512]{2,1,0:T(8,128)(2,1)S(1)}, bf16[2,2048,512]{2,1,0:T(8,128)(2,1)}, u32[]{:S(2)}) copy-start(bf16[2,2048,512]{2,1,0:T(8,128)(2,1)} %gate_ref.3) | copy-start | bytes 12582916
  83.7 82.4 %copy-start.2 = (bf16[2,2048,512]{2,1,0:T(8,128)(2,1)S(1)}, bf16[2,2048,512]{2,1,0:T(8,128)(2,1)}, u32[]{:S(2)}) copy-start(bf16[2,2048,512]{2,1,0:T(8,128)(2,1)} %up_ref.1) | copy-start | bytes 12582916
  83.7 82.4 %copy-start.3 = (bf16[2,512,2048]{2,1,0:T(8,128)(2,1)S(1)}, bf16[2,512,2048]{2,1,0:T(8,128)(2,1)}, u32[]{:S(2)}) copy-start(bf16[2,512,2048]{2,1,0:T(8,128)(2,1)} %down_ref.1) | copy-start | bytes 12582916
  180.8 79.3 %copy-start.5 = (bf16[256,6144]{1,0:T(8,128)(2,1)S(1)}, bf16[256,6144]{1,0:T(8,128)(2,1)}, u32[]{:S(2)}) copy-start(bf16[256,6144]{1,0:T(8,128)(2,1)} %copy-done.4) | copy-start | bytes 9437188

commit v3 on v2

--- a/solution.py
+++ b/solution.py
@@ -67,10 +67,9 @@
 
 
 def fill_spread(ref):
-    width = (SUB - 1) * BLK
-    src = iota((BLK, width), 0)
-    dst = iota((BLK, width), 1)
-    ref[...] = (src == SUB * ((dst % BLK) // SUB) + dst // BLK).astype(bf16)
+    ahead = iota((BLK, BLK), 0) - SUB * (iota((BLK, BLK), 1) // SUB)
+    for j in range(SUB - 1):
+        ref[:, j * BLK : (j + 1) * BLK] = (ahead == j).astype(bf16)
 
 
 def inverses(couplings, spread_ref):
@@ -171,7 +170,7 @@
             ks[b, c] = unit[b * BLK : (b + 1) * BLK]
             kb = split(ks[b, c])
             grams[b, c] = dot3(kb, kb, NT)
-            scores[b, c] = dot(qs[b, c].astype(bf16), kb[0], NT)
+            scores[b, c] = dot3(split(qs[b, c]), kb, NT)
     for n, (b, i) in enumerate(keyed):
         spread = tall[:, 2 * n : 2 * n + 1] - rows[b, i][0]
         masks[b, i] = jnp.where(row >= col, jnp.exp(jnp.where(row >= col, spread, 0.0)), 0.0)
@@ -186,13 +185,13 @@
         vb = values[b * BLK : (b + 1) * BLK, i * HD : (i + 1) * HD]
         grow = jnp.exp(cum_c)
         last = cum_c[BLK - 1 : BLK, :]
-        key_tail = (kb * jnp.exp(last - cum_c)).astype(bf16)
+        key_tail = split(kb * jnp.exp(last - cum_c))
         rhs = jnp.concatenate([beta_c * vb, (beta_c * grow) * kb], axis=1)
-        solved = dot3(invs[n], split(rhs)).astype(bf16)
-        near = dot((scores[b, i // 2] * masks[b, i]).astype(bf16), solved)
+        solved = split(dot3(invs[n], split(rhs)))
+        near = dot3(split(scores[b, i // 2] * masks[b, i]), solved)
         local = near[:, :HD]
         lift = grow * qb - near[:, HD:]
-        both = dot(solved, key_tail, TN)
+        both = dot3(solved, key_tail, TN)
         res[b, i] = (local, lift, jnp.exp(last), both)
     for i in range(heads):
         l0, f0, t0, both0 = res[0, i]
@@ -460,7 +459,7 @@
                 x_ref[e, pl.ds(2 * PR * i, 2 * PR), q * QW : (q + 1) * QW] = both
         return 0
 
-    lax.fori_loop(0, pairs, load, 0, unroll=4)
+    lax.fori_loop(0, pairs, load, 0, unroll=16)
     for e in range(2):
         x = x_ref[e]
         g = dot(x, gate_ref[e])
@@ -480,7 +479,7 @@
             out_ref[pl.ds(2 * GR * i + GR * h, GR), :] = dot(perm_t, z).astype(bf16)
         return 0
 
-    lax.fori_loop(0, pairs, store, 0, unroll=4)
+    lax.fori_loop(0, pairs, store, 0, unroll=16)
 
 
 def experts_mlp(arrived, gate, up, down):

time: 263 us -> 262 us (level)
  no operation moved by 1% of the time
where the time goes in v3:
time: 262 us
  blocking collectives  188 us (72%)
  Pallas kernels  41.2 us (16%)
  starting transfers between devices  17.5 us (7%)
  waiting for transfers between devices  11.7 us (4%)
    all_to_all x2, blocking collectives, exchange(): lax.all_to_all(chunks, ('seq', 'exp'), split_axis=0, concat_axis=0, tiled...  162 us
    all_to_all x2, blocking collectives, swap(): lax.all_to_all(array, 'seq', split_axis=0, concat_axis=0, axis_index_grou...  26.5 us
    pallas_call x1, Pallas kernels, mixer_blocks(): pl.pallas_call(mixer_body, grid=(4 // KH,), in_specs=[pl.BlockSpec((TOK,...  14.6 us
    pallas_call x1, Pallas kernels, experts_mlp(): pl.pallas_call(expert_body, in_specs=in_vmem(4), out_shape=jax.ShapeDtype...  13.3 us
    all_to_all x1, waiting for transfers between devices, body(): lax.all_to_all(parts, 'exp', split_axis=0, concat_axis=0, tiled=True)  9.1 us
    ppermute x3, starting transfers between devices, body(): lax.ppermute(total, 'seq', [(s, s + k * NEAR) for s in range(SEQ - k * NE...  8.61 us
  transfers between devices with their start and end apart: 5, of which 3 were waited for; matrix products, arithmetic and copies ran while one was open for 0% of the time, Pallas kernels for 1%

profile of v3, /device:TPU:1, one launch (start us, length us, event | category | flops | bytes accessed | tf_op | source)
XLA Modules:
  0.0 262.0 jit_solution(7273379950173250486)
XLA Ops:
  0.6 1.4 edge_rows.1
  2.0 4.9 %collective-permute-start = (bf16[8,2048]{1,0:T(8,128)(2,1)}, bf16[8,2048]{1,0:T(8,128)(2,1)S(1)}, u32[]{:S(2)}, u32[]{:S(2)}) collective-permute-start(bf16[8,2048]{1,0:T(8,128)(2,1)} %edge_rows.1), channel_id=1, source_target_pairs={{0,4},{4,8},{8,12},{12,16},{16,20},{20,24},{24,28},{28,32},{32,36}... | collective-permute-start | bytes 98312 | tf_op jit(solution)/shard_map/ppermute | solution.py:543
  6.9 1.3 collective-permute-done.halo_ref
  8.2 0.0 copy-start.12
  8.2 0.6 copy-done.12
  8.9 0.0 copy-start
  8.9 0.0 copy-start.7
  8.9 0.0 copy-start.11
  8.9 14.6 %mixer_blocks.1 = (bf16[8,256,128]{2,1,0:T(8,128)(2,1)}, f32[8,256,128]{2,1,0:T(8,128)}, bf16[8,256,128]{2,1,0:T(8,128)(2,1)}) custom-call(bf16[256,512]{1,0:T(8,128)(2,1)} %q_ref.3, bf16[256,512]{1,0:T(8,128)(2,1)} %k_ref.3, bf16[256,1024]{1,0:T(8,128)(2,1)} %v_ref.3, bf16[8,2048]{1,0:T(8,128)(2,1)} %copy-done.12, f32[8,256]{1,0:T(8,128)} %bitcast.15, ...), custom_call_target="tpu_custom_call" | custom-call | tf_op jit(solution)/shard_map/mixer_blocks/pallas_call | solution.py:218
  23.4 0.0 copy-start.6
  23.4 0.0 copy-start.8
  23.4 15.5 %all_to_all.25.in_ref = bf16[8,256,128]{2,1,0:T(8,128)(2,1)S(1)} all-to-all(bf16[8,256,128]{2,1,0:T(8,128)(2,1)} %get-tuple-element.12), channel_id=1, replica_groups={{0,4,8,12,16,20,24,28},{32,36,40,44,48,52,56,60},{64,68,72,76,80,84,88,..., dimensions={0} | all-to-all | bytes 1048576 | tf_op jit(solution)/shard_map/all_to_all | solution.py:560
  38.9 1.1 near_scan.1
  40.0 4.8 %collective-permute-start.3 = (bf16[256,128]{1,0:T(8,128)(2,1)S(1)}, bf16[256,128]{1,0:T(8,128)(2,1)S(1)}, u32[]{:S(2)}, u32[]{:S(2)}) collective-permute-start(bf16[256,128]{1,0:T(8,128)(2,1)S(1)} %get-tuple-element.13), channel_id=1, source_target_pairs={{0,96},{4,100},{8,104},{12,108},{16,112},{20,116},{24,120},{28,124... | collective-permute-start | bytes 196616 | tf_op jit(solution)/shard_map/ppermute | solution.py:564
  44.9 1.3 collective-permute-start.2
  46.2 2.5 collective-permute-start.1
  48.7 0.0 collective-permute-done.3.last_ref
  48.7 0.0 collective-permute-done.2.next_ref
  48.7 1.3 collective-permute-done.1.near_ref
  50.0 0.6 far_scan.1
  50.5 11.1 %all_to_all.26.s_ref = bf16[8,128,128]{2,1,0:T(8,128)(2,1)S(1)} all-to-all(bf16[8,128,128]{2,1,0:T(8,128)(2,1)S(1)} %far_scan.1), channel_id=1, replica_groups={{0,4,8,12,16,20,24,28},{32,36,40,44,48,52,56,60},{64,68,72,76,80,84,88,..., dimensions={0} | all-to-all | bytes 524288 | tf_op jit(solution)/shard_map/all_to_all | solution.py:560
  61.6 0.0 copy-done
  61.6 0.0 copy-done.7
  61.6 0.0 copy-done.11
  61.6 0.0 copy-done.6
  61.6 0.0 copy-done.8
  61.6 0.0 copy-start.13
  61.6 0.0 copy-start.14
  61.6 0.0 copy-start.9
  61.7 0.0 copy-start.10
  61.7 2.8 %project.1 = bf16[4,64,2048]{2,1,0:T(8,128)(2,1)} custom-call(bf16[8,128,128]{2,1,0:T(8,128)(2,1)S(1)} %all_to_all.26.s_ref, f32[8,256,128]{2,1,0:T(8,128)S(1)} %copy-done.6, bf16[8,256,128]{2,1,0:T(8,128)(2,1)S(1)} %copy-done.8, bf16[256,1024]{1,0:T(8,128)(2,1)S(1)} %copy-done.7, f32[1,128]{1,0:T(1,128)S(1)} %bitcast.14, bf16[1024,2048]{1,0:T(8,128)(2,1)S(1)} %copy-done), custom_call_target="tpu_custom_call" | custom-call | tf_op jit(solution)/shard_map/project/pallas_call | solution.py:341
  64.4 4.0 %all-to-all-start.2 = ((bf16[4,64,2048]{2,1,0:T(8,128)(2,1)}), bf16[4,64,2048]{2,1,0:T(8,128)(2,1)S(1)}, u32[]{:S(2)}, u32[]{:S(2)}) async-start(bf16[4,64,2048]{2,1,0:T(8,128)(2,1)} %project.1), calls=%async_computation.2 | async-start | bytes 2097152 | tf_op jit(solution)/shard_map/all_to_all | solution.py:570
  68.4 0.0 copy-done.13
  68.4 0.1 copy.21.experts_ref
  68.5 0.0 copy-done.14
  68.5 0.1 copy.22.weights_ref
  68.6 2.9 %route.1 = (f32[48,128]{1,0:T(8,128)S(1)}, bf16[256,6144]{1,0:T(8,128)(2,1)S(1)}) custom-call(s32[64,10]{1,0:T(8,128)S(1)} %copy.21.experts_ref, f32[64,10]{1,0:T(8,128)S(1)} %copy.22.weights_ref), custom_call_target="tpu_custom_call" | custom-call | tf_op jit(solution)/shard_map/route/pallas_call | solution.py:387
  71.6 0.0 copy-start.4
  71.6 1.6 copy-done.4
  73.2 9.1 %all-to-all-done.2.parts_ref = bf16[4,64,2048]{2,1,0:T(8,128)(2,1)S(1)} async-done(((bf16[4,64,2048]{2,1,0:T(8,128)(2,1)}), bf16[4,64,2048]{2,1,0:T(8,128)(2,1)S(1)}, u32[]{:S(2)}, u32[]{:S(2)}) %all-to-all-start.2) | async-done | bytes 1048608 | tf_op jit(solution)/shard_map/all_to_all | solution.py:570
  82.3 0.0 copy-done.9
  82.3 0.0 copy-done.10
  82.3 2.1 dispatch.1
  84.4 0.0 copy-start.1
  84.4 0.0 copy-start.2
  84.5 0.0 copy-start.3
  84.5 82.4 %all_to_all.27 = bf16[128,48,512]{2,1,0:T(8,128)(2,1)S(1)} all-to-all(bf16[128,48,512]{2,1,0:T(8,128)(2,1)S(1)} %bitcast.12), channel_id=1, replica_groups=mesh['seq'=32,'exp'=4] {'seq','exp'}, dimensions={0} | all-to-all | bytes 12582912 | tf_op jit(solution)/shard_map/all_to_all | solution.py:517
  166.8 0.0 copy-done.1
  166.9 0.0 copy-done.2
  166.9 0.0 copy-done.3
  166.9 13.3 %experts_mlp.1 = bf16[6144,512]{1,0:T(8,128)(2,1)S(1)} custom-call(bf16[6144,512]{1,0:T(8,128)(2,1)S(1)} %bitcast.10, bf16[2,2048,512]{2,1,0:T(8,128)(2,1)S(1)} %copy-done.1, bf16[2,2048,512]{2,1,0:T(8,128)(2,1)S(1)} %copy-done.2, bf16[2,512,2048]{2,1,0:T(8,128)(2,1)S(1)} %copy-done.3), custom_call_target="tpu_custom_call" | custom-call | tf_op jit(solution)/shard_map/experts_mlp/pallas_call | solution.py:486
  180.2 0.0 copy-start.5
  180.2 79.3 %all_to_all.28 = bf16[128,48,512]{2,1,0:T(8,128)(2,1)S(1)} all-to-all(bf16[128,48,512]{2,1,0:T(8,128)(2,1)S(1)} %bitcast.11), channel_id=1, replica_groups=mesh['seq'=32,'exp'=4] {'seq','exp'}, dimensions={0} | all-to-all | bytes 12582912 | tf_op jit(solution)/shard_map/all_to_all | solution.py:517
  259.5 0.0 copy-done.5
  259.5 2.5 combine.1
Async XLA Ops:
  2.0 6.2 %collective-permute-start = (bf16[8,2048]{1,0:T(8,128)(2,1)}, bf16[8,2048]{1,0:T(8,128)(2,1)S(1)}, u32[]{:S(2)}, u32[]{:S(2)}) collective-permute-start(bf16[8,2048]{1,0:T(8,128)(2,1)} %edge_rows.1), channel_id=1, source_target_pairs={{0,4},{4,8},{8,12},{12,16},{16,20},{20,24},{24,28},{28,32},{32,36}... | collective-permute-start | bytes 98312 | tf_op jit(solution)/shard_map/ppermute | solution.py:543
  8.2 0.6 copy-start.12
  8.9 52.7 %copy-start = (bf16[1024,2048]{1,0:T(8,128)(2,1)S(1)}, bf16[1024,2048]{1,0:T(8,128)(2,1)}, u32[]{:S(2)}) copy-start(bf16[1024,2048]{1,0:T(8,128)(2,1)} %w_ref.3) | copy-start | bytes 12582916
  8.9 52.7 %copy-start.7 = (bf16[256,1024]{1,0:T(8,128)(2,1)S(1)}, bf16[256,1024]{1,0:T(8,128)(2,1)}, u32[]{:S(2)}) copy-start(bf16[256,1024]{1,0:T(8,128)(2,1)} %gate_ref.2) | copy-start | bytes 1572868
  8.9 52.7 %copy-start.11 = (f32[128]{0:T(128)S(1)}, f32[128]{0:T(128)}, u32[]{:S(2)}) copy-start(f32[128]{0:T(128)} %param.29) | copy-start | bytes 1540
  23.4 38.2 %copy-start.6 = (f32[8,256,128]{2,1,0:T(8,128)S(1)}, f32[8,256,128]{2,1,0:T(8,128)}, u32[]{:S(2)}) copy-start(f32[8,256,128]{2,1,0:T(8,128)} %get-tuple-element.16.local_ref) | copy-start | bytes 3145732
  23.4 38.2 %copy-start.8 = (bf16[8,256,128]{2,1,0:T(8,128)(2,1)S(1)}, bf16[8,256,128]{2,1,0:T(8,128)(2,1)}, u32[]{:S(2)}) copy-start(bf16[8,256,128]{2,1,0:T(8,128)(2,1)} %get-tuple-element.17.lift_ref) | copy-start | bytes 1572868
  40.0 8.6 %collective-permute-start.3 = (bf16[256,128]{1,0:T(8,128)(2,1)S(1)}, bf16[256,128]{1,0:T(8,128)(2,1)S(1)}, u32[]{:S(2)}, u32[]{:S(2)}) collective-permute-start(bf16[256,128]{1,0:T(8,128)(2,1)S(1)} %get-tuple-element.13), channel_id=1, source_target_pairs={{0,96},{4,100},{8,104},{12,108},{16,112},{20,116},{24,120},{28,124... | collective-permute-start | bytes 196616 | tf_op jit(solution)/shard_map/ppermute | solution.py:564
  44.9 3.8 %collective-permute-start.2 = (bf16[256,128]{1,0:T(8,128)(2,1)S(1)}, bf16[256,128]{1,0:T(8,128)(2,1)S(1)}, u32[]{:S(2)}, u32[]{:S(2)}) collective-permute-start(bf16[256,128]{1,0:T(8,128)(2,1)S(1)} %get-tuple-element.13), channel_id=1, source_target_pairs={{0,64},{4,68},{8,72},{12,76},{16,80},{20,84},{24,88},{28,92},{32,9... | collective-permute-start | bytes 196616 | tf_op jit(solution)/shard_map/ppermute | solution.py:564
  46.2 3.8 %collective-permute-start.1 = (bf16[256,128]{1,0:T(8,128)(2,1)S(1)}, bf16[256,128]{1,0:T(8,128)(2,1)S(1)}, u32[]{:S(2)}, u32[]{:S(2)}) collective-permute-start(bf16[256,128]{1,0:T(8,128)(2,1)S(1)} %get-tuple-element.13), channel_id=1, source_target_pairs={{0,32},{4,36},{8,40},{12,44},{16,48},{20,52},{24,56},{28,60},{32,6... | collective-permute-start | bytes 196616 | tf_op jit(solution)/shard_map/ppermute | solution.py:564
  61.6 6.8 %copy-start.13 = (s32[64,10]{0,1:T(8,128)S(1)}, s32[64,10]{0,1:T(8,128)}, u32[]{:S(2)}) copy-start(s32[64,10]{0,1:T(8,128)} %param.33) | copy-start | bytes 7684
  61.6 6.9 %copy-start.14 = (f32[64,10]{0,1:T(8,128)S(1)}, f32[64,10]{0,1:T(8,128)}, u32[]{:S(2)}) copy-start(f32[64,10]{0,1:T(8,128)} %param.34) | copy-start | bytes 7684
  61.6 20.7 %copy-start.9 = (bf16[64,2048]{1,0:T(8,128)(2,1)S(1)}, bf16[64,2048]{1,0:T(8,128)(2,1)}, u32[]{:S(2)}) copy-start(bf16[64,2048]{1,0:T(8,128)(2,1)} %res_ref.1) | copy-start | bytes 786436
  61.7 20.6 %copy-start.10 = (f32[2048]{0:T(1024)S(1)}, f32[2048]{0:T(1024)}, u32[]{:S(2)}) copy-start(f32[2048]{0:T(1024)} %param.32) | copy-start | bytes 24580
  64.4 17.9 %all-to-all-start.2 = ((bf16[4,64,2048]{2,1,0:T(8,128)(2,1)}), bf16[4,64,2048]{2,1,0:T(8,128)(2,1)S(1)}, u32[]{:S(2)}, u32[]{:S(2)}) async-start(bf16[4,64,2048]{2,1,0:T(8,128)(2,1)} %project.1), calls=%async_computation.2 | async-start | bytes 2097152 | tf_op jit(solution)/shard_map/all_to_all | solution.py:570
  71.6 1.6 copy-start.4
  84.4 82.4 %copy-start.1 = (bf16[2,2048,512]{2,1,0:T(8,128)(2,1)S(1)}, bf16[2,2048,512]{2,1,0:T(8,128)(2,1)}, u32[]{:S(2)}) copy-start(bf16[2,2048,512]{2,1,0:T(8,128)(2,1)} %gate_ref.3) | copy-start | bytes 12582916
  84.4 82.4 %copy-start.2 = (bf16[2,2048,512]{2,1,0:T(8,128)(2,1)S(1)}, bf16[2,2048,512]{2,1,0:T(8,128)(2,1)}, u32[]{:S(2)}) copy-start(bf16[2,2048,512]{2,1,0:T(8,128)(2,1)} %up_ref.1) | copy-start | bytes 12582916
  84.5 82.4 %copy-start.3 = (bf16[2,512,2048]{2,1,0:T(8,128)(2,1)S(1)}, bf16[2,512,2048]{2,1,0:T(8,128)(2,1)}, u32[]{:S(2)}) copy-start(bf16[2,512,2048]{2,1,0:T(8,128)(2,1)} %down_ref.1) | copy-start | bytes 12582916
  180.2 79.3 %copy-start.5 = (bf16[256,6144]{1,0:T(8,128)(2,1)S(1)}, bf16[256,6144]{1,0:T(8,128)(2,1)}, u32[]{:S(2)}) copy-start(bf16[256,6144]{1,0:T(8,128)(2,1)} %copy-done.4) | copy-start | bytes 9437188
